TPU v7x, 32 devices: a whole 2x2x4 slice. The times are simulated.
32 devices in a mesh: gx: 8 (over y, x, core), gy: 4 (over z).
Axes of the slice: x: 2, y: 2, z: 4, core: 2. Of those that a mesh axis runs over, the one named last changes fastest.
Arguments:
- object_field: float32 [2, 2048, 4096], P(None, 'gy', 'gx'), may hold values from -6 to 6
- probe: float32 [3, 2, 256, 256], replicated, may hold values from -6 to 6
- positions: int32 [4, 8, 4, 2], P('gy', 'gx'), may hold values from 0 to 512
- frame_count: int32 [4, 8], P('gy', 'gx'), may hold values from 1 to 4, as said below
- measured: float32 [4, 8, 4, 256, 256], P('gy', 'gx'), may hold values from 0.5 to 20
Outputs:
- object_grad: float32 [2, 2048, 4096], P(None, 'gy', 'gx')
Inputs may be any that keep to these rules, and one draw needn't show every extreme that they name: `frame_count`: some tile has all 4 slots live in every draw; live frames fill the first slots of a tile; tiles in the columns tx >= 4 have exactly 1 live frame.
All inputs are finite; a program needn't handle non-finite values.
Results may differ from a plain program's by a relative error of at most 0.0045.
Values sent between devices are 32-bit elements; how exact they have to be, the bound alone decides.
No kernel may reach another device: no remote copies, remote signals or barrier semaphores. Data moves between devices by JAX's collectives and lax.ppermute only.
A program may use at most 64 MiB of HBM per device.

v0:
```python
import functools
import math

import jax
import jax.numpy as jnp
import numpy as np
from jax import lax
from jax.experimental import pallas as pl
from jax.experimental.pallas import tpu as pltpu
from jax.sharding import PartitionSpec as P


HALO = 128
LANE = 128
F32 = jnp.float32
BF16 = jnp.bfloat16
ANY = pl.BlockSpec(memory_space=pl.ANY)
VM = pl.BlockSpec(memory_space=pltpu.VMEM)
SM = pl.BlockSpec(memory_space=pltpu.SMEM)
HB = pl.BlockSpec(memory_space=pltpu.HBM)


def dft_tables(width):
    half = width // 2
    t = np.arange(width)
    order = np.concatenate([t[0::2], t[1::2]])
    phase = 2.0 * math.pi / width * np.mod(np.outer(t, order), width)
    c = np.cos(phase) / math.sqrt(width)
    s = np.sin(phase) / math.sqrt(width)
    blocks, small = [], []
    for b in (slice(0, half), slice(half, width)):
        blocks += [np.concatenate([c[:, b], s[:, b]]), np.concatenate([-s[:, b], c[:, b]])]
        ct, st = c[:half, b].T, s[:half, b].T
        small.append(np.block([[ct, st], [-st, ct]]))
    fwd = np.concatenate(blocks, axis=1)
    big = np.stack([fwd, fwd.T])
    small = np.stack(small + [m.T for m in small])
    return jnp.asarray(big, BF16), jnp.asarray(small, BF16)


def dot(a, b):
    return jnp.dot(a, b, preferred_element_type=F32)


def rows_kernel(own, to_up, to_down, sem):
    rows = own.shape[1]
    copies = [
        pltpu.make_async_copy(own.at[:, pl.ds(rows - HALO, HALO), :], to_down, sem.at[0]),
        pltpu.make_async_copy(own.at[:, pl.ds(0, HALO), :], to_up, sem.at[1]),
    ]
    for cp in copies:
        cp.start()
    for cp in copies:
        cp.wait()


def edges_kernel(info, own, edge_e, edge_o, sem):
    far = own.shape[2] - HALO
    odd = info[0, 0]
    start_e = pl.multiple_of(jnp.where(odd == 1, 0, far), LANE)
    start_o = pl.multiple_of(jnp.where(odd == 1, far, 0), LANE)
    copies = [
        pltpu.make_async_copy(own.at[:, :, pl.ds(start_e, HALO)], edge_e, sem.at[0]),
        pltpu.make_async_copy(own.at[:, :, pl.ds(start_o, HALO)], edge_o, sem.at[1]),
    ]
    for cp in copies:
        cp.start()
    for cp in copies:
        cp.wait()


def corners_kernel(info, up, down, corner_e, corner_o):
    far = up.shape[2] - HALO
    odd = info[0, 0]
    start_e = pl.multiple_of(jnp.where(odd == 1, 0, far), LANE)
    start_o = pl.multiple_of(jnp.where(odd == 1, far, 0), LANE)
    for i, strip in enumerate((up, down)):
        corner_e[i] = strip[:, :, pl.ds(start_e, HALO)]
        corner_o[i] = strip[:, :, pl.ds(start_o, HALO)]


def prepare_kernel(measured_h, own, probe, big, small, amp, ext, acc, probe_v, big_v, small_v, measured, sem):
    slots, width, _ = measured.shape
    half = width // 2
    rows = own.shape[1]
    blocks = own.shape[2] // LANE
    copies = [(measured_h, measured), (probe, probe_v), (big, big_v), (small, small_v)]
    for b in range(blocks):
        copies.append((own.at[:, :, pl.ds(b * LANE, LANE)], ext.at[:, b + 1, pl.ds(HALO, rows)]))
    copies = [pltpu.make_async_copy(p, q, sem.at[i]) for i, (p, q) in enumerate(copies)]
    for cp in copies:
        cp.start()
    acc[...] = jnp.zeros_like(acc)
    i = lax.broadcasted_iota(jnp.int32, (width, width), 0)
    j = lax.broadcasted_iota(jnp.int32, (width, width), 1)
    source = jnp.where(j < half, 2 * j, 2 * (j - half) + 1)
    cols = (i == source).astype(F32)
    source = jnp.where(i < half, 2 * i, 2 * (i - half) + 1)
    perm = (j == source).astype(F32)
    copies[0].wait()
    for k in range(slots):
        a = jnp.sqrt(measured[k])
        a = jnp.dot(perm, a, precision=lax.Precision.HIGHEST, preferred_element_type=F32)
        amp[k] = jnp.dot(a, cols, precision=lax.Precision.HIGHEST, preferred_element_type=F32)
    for cp in copies[1:]:
        cp.wait()


def one_frame(slot, info, ext, acc, probe, amp, big, small, patch, x, y, xa, xb, u, v, wave, factor):
    modes, _, width, _ = probe.shape
    h = width // 2
    chunk = 64
    lo, hi = slice(0, h), slice(h, width)
    r = info[0, 2 + 2 * slot]
    c = info[0, 3 + 2 * slot]
    q = jnp.minimum(c // LANE, ext.shape[1] - 3)
    s = c - q * LANE
    left = jnp.bitwise_and(LANE - s, LANE - 1)
    right = jnp.bitwise_and(s, LANE - 1)
    lane = lax.broadcasted_iota(jnp.int32, (chunk, LANE), 1)
    keep = lane < LANE - s
    for ch in range(2):
        for i in range(0, width, chunk):
            rows = pl.ds(r + i, chunk)
            rot = [pltpu.roll(ext[ch, q + t, rows, :], left, 1) for t in range(3)]
            patch[ch, i : i + chunk, lo] = jnp.where(keep, rot[0], rot[1])
            patch[ch, i : i + chunk, hi] = jnp.where(keep, rot[1], rot[2])
    for m in range(modes):
        for i in range(0, width, chunk):
            rows = slice(i, i + chunk)
            for cc in (lo, hi):
                pr, pi = probe[m, 0, rows, cc], probe[m, 1, rows, cc]
                o_re, o_im = patch[0, rows, cc], patch[1, rows, cc]
                x[m, rows, cc] = (pr * o_re - pi * o_im).astype(BF16)
                x[m, rows, slice(width + cc.start, width + cc.stop)] = (pr * o_im + pi * o_re).astype(BF16)
        for k in range(2):
            e = dot(x[m], big[0, :, k * width : (k + 1) * width])
            y[m, 0:width, k * h : (k + 1) * h] = e[:, lo].astype(BF16)
            y[m, width:, k * h : (k + 1) * h] = e[:, hi].astype(BF16)
    for m in range(modes):
        for k in range(2):
            p = dot(big[1, k * width : (k + 1) * width], y[m])
            wave[m, k] = p
            square = p[lo] * p[lo] + p[hi] * p[hi]
            factor[k] = square if m == 0 else factor[k] + square
    for k in range(2):
        factor[k] = 1.0 - amp[slot, k * h : (k + 1) * h, :] * lax.rsqrt(factor[k] + 1.0)
    for m in range(modes):
        for k in range(2):
            f = factor[k]
            for part in (lo, hi):
                w = f * wave[m, k, part, :]
                xa[m, k * h : (k + 1) * h, part] = w[:, lo].astype(BF16)
                xb[m, k * h : (k + 1) * h, part] = w[:, hi].astype(BF16)
    for m in range(modes):
        a, b = dot(xa[m], small[0]), dot(xb[m], small[1])
        for cc, z in ((lo, a + b), (hi, a - b)):
            for part in (lo, hi):
                u[m, part, cc] = z[lo, part].astype(BF16)
                v[m, part, cc] = z[hi, part].astype(BF16)
    for m in range(modes):
        a, b = dot(small[2], u[m]), dot(small[3], v[m])
        for rows, z in ((lo, a + b), (hi, a - b)):
            pr, pi = probe[m, 0, rows, :], probe[m, 1, rows, :]
            g_re = pr * z[lo] + pi * z[hi]
            g_im = pr * z[hi] - pi * z[lo]
            if m > 0:
                g_re = g_re + patch[0, rows, :]
                g_im = g_im + patch[1, rows, :]
            patch[0, rows, :] = g_re
            patch[1, rows, :] = g_im
    first = lane < s
    for ch in range(2):
        for i in range(0, width, chunk):
            rows = pl.ds(r + i, chunk)
            g0 = pltpu.roll(patch[ch, i : i + chunk, lo], right, 1)
            g1 = pltpu.roll(patch[ch, i : i + chunk, hi], right, 1)
            zero = jnp.zeros_like(g0)
            acc[ch, q, rows, :] += jnp.where(first, zero, g0)
            acc[ch, q + 1, rows, :] += jnp.where(first, g0, g1)
            acc[ch, q + 2, rows, :] += jnp.where(first, g1, zero)


def frame_stage(slot, info, odd, cols, width):
    c = info[0, 3 + 2 * slot]
    needs_right = c > cols + HALO - width
    needs_left = c < HALO
    return jnp.where(jnp.where(odd == 1, needs_right, needs_left), 1, 0)


def run_frames(stage, info, ext, acc, probe, amp, big, small, *scratch):
    width = probe.shape[-1]
    cols = (ext.shape[1] - 2) * LANE

    def step(slot, carry):
        @pl.when(frame_stage(slot, info, info[0, 0], cols, width) == stage)
        def _():
            one_frame(slot, info, ext, acc, probe, amp, big, small, *scratch)

        return carry

    lax.fori_loop(0, info[0, 1], step, 0)


def copy_all(pairs, sem):
    copies = [pltpu.make_async_copy(a, b, sem.at[i]) for i, (a, b) in enumerate(pairs)]
    for cp in copies:
        cp.start()
    for cp in copies:
        cp.wait()


def near_kernel(info, up, down, in_e, c_e, probe, amp, big, small, ext_in, acc_in, ext, acc, *rest):
    *scratch, sem = rest
    blocks = ext.shape[1] - 2
    rows = ext.shape[2] - 2 * HALO
    col_e = jnp.where(info[0, 0] == 1, 0, blocks + 1)
    top, mid, low = pl.ds(0, HALO), pl.ds(HALO, rows), pl.ds(HALO + rows, HALO)
    pairs = []
    for b in range(blocks):
        lanes = pl.ds(b * LANE, LANE)
        pairs.append((up.at[:, :, lanes], ext.at[:, b + 1, top]))
        pairs.append((down.at[:, :, lanes], ext.at[:, b + 1, low]))
    pairs += [(in_e, ext.at[:, col_e, mid]), (c_e.at[0], ext.at[:, col_e, top]), (c_e.at[1], ext.at[:, col_e, low])]
    copy_all(pairs, sem)
    run_frames(0, info, ext, acc, probe, amp, big, small, *scratch)


def outer_kernel(info, in_o, c_o, probe, amp, big, small, ext_in, acc_in,
                 ext, acc, rim_e, rim_o, rim_top, rim_low, *rest):
    *scratch, sem = rest
    blocks = ext.shape[1] - 2
    rows = ext.shape[2] - 2 * HALO
    odd = info[0, 0]
    col_e = jnp.where(odd == 1, 0, blocks + 1)
    col_o = jnp.where(odd == 1, blocks + 1, 0)
    top, mid, low = pl.ds(0, HALO), pl.ds(HALO, rows), pl.ds(HALO + rows, HALO)
    copy_all([(in_o, ext.at[:, col_o, mid]), (c_o.at[0], ext.at[:, col_o, top]), (c_o.at[1], ext.at[:, col_o, low])], sem)
    run_frames(1, info, ext, acc, probe, amp, big, small, *scratch)
    for ch in range(2):
        rim_e[ch] = acc[ch, col_e]
        rim_top[ch] = acc[ch, col_o, 0:HALO]
        rim_o[ch] = acc[ch, col_o, HALO : HALO + rows]
        rim_low[ch] = acc[ch, col_o, HALO + rows :]


def rims_kernel(info, acc, in_e, to_up, to_down):
    blocks = acc.shape[1] - 2
    rows = acc.shape[2]
    odd = info[0, 0]
    block_e = jnp.where(odd == 1, 0, blocks - 1)
    top, low = slice(0, HALO), slice(rows - HALO, rows)
    to_up[...] = acc[:, 1 : blocks + 1, top, :]
    to_down[...] = acc[:, 1 : blocks + 1, low, :]
    for ch in range(2):
        to_up[ch, block_e] += in_e[ch, top]
        to_down[ch, block_e] += in_e[ch, low]


def join_kernel(info, acc, in_e, in_o, from_above, from_below, c_above, c_below, out, buf, sem):
    blocks = acc.shape[1] - 2
    rows = acc.shape[2] - 2 * HALO
    odd = info[0, 0]
    block_e = jnp.where(odd == 1, 0, blocks - 1)
    block_o = jnp.where(odd == 1, blocks - 1, 0)
    top, low = slice(0, HALO), slice(rows - HALO, rows)
    for b in range(blocks):
        buf[:, b] = acc[:, b + 1, HALO : HALO + rows, :]
        buf[:, b, top] += from_above[:, b]
        buf[:, b, low] += from_below[:, b]
    for ch in range(2):
        buf[ch, block_e] += in_e[ch, HALO : HALO + rows]
        buf[ch, block_o] += in_o[ch]
        buf[ch, block_o, top] += c_above[ch]
        buf[ch, block_o, low] += c_below[ch]
    copies = [pltpu.make_async_copy(buf.at[:, b], out.at[:, :, pl.ds(b * LANE, LANE)], sem.at[b]) for b in range(blocks)]
    for cp in copies:
        cp.start()
    for cp in copies:
        cp.wait()


def call(kernel, in_specs, out_specs, out_shape, scratch=(), limit=8 << 20, flops=0, moved=0, aliases=None):
    return pl.pallas_call(
        kernel,
        in_specs=in_specs,
        out_specs=out_specs,
        out_shape=out_shape,
        scratch_shapes=scratch,
        input_output_aliases=aliases or {},
        compiler_params=pltpu.CompilerParams(vmem_limit_bytes=limit),
        cost_estimate=pl.CostEstimate(flops=flops, bytes_accessed=moved, transcendentals=0),
    )


def program(object_field, probe, positions, frame_count, measured):
    width = probe.shape[-1]
    modes = probe.shape[0]
    _, rows, cols = object_field.shape
    blocks = cols // LANE
    n_gx = lax.axis_size("gx")
    n_gy = lax.axis_size("gy")
    slots = measured.shape[2]
    odd = (lax.axis_index("gx") % 2).astype(jnp.int32)
    info = jnp.concatenate([odd.reshape(1), frame_count.reshape(1), positions.reshape(2 * slots)]).reshape(1, -1)
    object_field, probe, measured = [pltpu.with_memory_space_constraint(a, pltpu.HBM) for a in (object_field, probe, measured[0, 0])]
    pairs_e = [(i, i ^ 1) for i in range(n_gx) if i ^ 1 < n_gx]
    pairs_o = [(i, i + 1) for i in range(1, n_gx - 1, 2)]
    pairs_o += [(j, i) for i, j in pairs_o]
    pairs_down = [(i, i + 1) for i in range(n_gy - 1)]
    pairs_up = [(j, i) for i, j in pairs_down]

    def diagonal(pairs):
        return [(i * n_gy + z, j * n_gy + w) for z, w in pairs for i, j in pairs_o]

    shape = functools.partial(jax.ShapeDtypeStruct, dtype=F32)
    vmem = pltpu.VMEM
    dma = pltpu.SemaphoreType.DMA
    big, small = [pltpu.with_memory_space_constraint(a, pltpu.HBM) for a in dft_tables(width)]

    strip = shape((2, HALO, cols))
    to_up, to_down = call(rows_kernel, [HB], [VM] * 2, [strip] * 2, [dma((2,))])(object_field)
    up = lax.ppermute(to_down, "gy", pairs_down)
    down = lax.ppermute(to_up, "gy", pairs_up)
    edge = shape((2, rows, HALO))
    edge_e, edge_o = call(edges_kernel, [SM, HB], [VM] * 2, [edge] * 2, [dma((2,))])(info, object_field)
    in_e = lax.ppermute(edge_e, "gx", pairs_e)
    in_o = lax.ppermute(edge_o, "gx", pairs_o)

    ext_shape = (2, blocks + 2, rows + 2 * HALO, LANE)
    amp, ext, acc, probe, big, small = call(
        prepare_kernel,
        [HB] * 5,
        [VM] * 6,
        [shape(measured.shape), shape(ext_shape), shape(ext_shape), shape(probe.shape),
         jax.ShapeDtypeStruct(big.shape, BF16), jax.ShapeDtypeStruct(small.shape, BF16)],
        [vmem(measured.shape, F32), dma((4 + blocks,))],
        limit=24 << 20,
        flops=10**9,
        moved=10**7,
    )(measured, object_field, probe, big, small)

    corner = shape((2, 2, HALO, HALO))
    corner_e, corner_o = call(corners_kernel, [SM, VM, VM], [VM] * 2, [corner] * 2)(info, up, down)
    c_e = lax.ppermute(corner_e, "gx", pairs_e)
    c_o = lax.ppermute(corner_o, "gx", pairs_o)

    work = [
        vmem((2, width, width), F32),
        vmem((modes, width, 2 * width), BF16),
        vmem((modes, 2 * width, width), BF16),
        vmem((modes, width, width), BF16),
        vmem((modes, width, width), BF16),
        vmem((modes, width, width), BF16),
        vmem((modes, width, width), BF16),
        vmem((modes, 2, width, width), F32),
        vmem((2, width // 2, width), F32),
        dma((2 * blocks + 3,)),
    ]
    ext, acc = call(
        near_kernel,
        [SM] + [ANY] * 4 + [VM] * 6,
        [VM] * 2,
        [shape(ext_shape)] * 2,
        work,
        limit=32 << 20,
        flops=10**10,
        moved=10**7,
        aliases={9: 0, 10: 1},
    )(info, up, down, in_e, c_e, probe, amp, big, small, ext, acc)
    piece = shape((2, HALO, HALO))
    _, acc, rim_e, rim_o, rim_top, rim_low = call(
        outer_kernel,
        [SM] + [ANY] * 2 + [VM] * 6,
        [VM] * 6,
        [shape(ext_shape)] * 2 + [shape((2, rows + 2 * HALO, HALO)), edge, piece, piece],
        work,
        limit=32 << 20,
        flops=10**10,
        moved=10**7,
        aliases={7: 0, 8: 1},
    )(info, in_o, c_o, probe, amp, big, small, ext, acc)

    back_e = lax.ppermute(rim_e, "gx", pairs_e)
    back_o = lax.ppermute(rim_o, "gx", pairs_o)
    strip = shape((2, blocks, HALO, LANE))
    to_up, to_down = call(rims_kernel, [SM, VM, VM], [VM] * 2, [strip] * 2)(info, acc, back_e)
    from_below = lax.ppermute(to_up, "gy", pairs_up)
    from_above = lax.ppermute(to_down, "gy", pairs_down)
    c_below = lax.ppermute(rim_top, ("gx", "gy"), diagonal(pairs_up))
    c_above = lax.ppermute(rim_low, ("gx", "gy"), diagonal(pairs_down))
    return call(
        join_kernel,
        [SM] + [VM] * 7,
        ANY,
        shape(object_field.shape),
        [vmem((2, blocks, rows, LANE), F32), dma((blocks,))],
        limit=16 << 20,
    )(info, acc, back_e, back_o, from_above, from_below, c_above, c_below)


def solution(mesh):
    return jax.shard_map(
        program,
        mesh=mesh,
        in_specs=(
            P(None, "gy", "gx"),
            P(),
            P("gy", "gx", None, None),
            P("gy", "gx"),
            P("gy", "gx", None, None, None),
        ),
        out_specs=P(None, "gy", "gx"),
        check_vma=False,
    )
```

profile of v0, /device:TPU:1, one launch (start us, length us, event | category | flops | bytes accessed | tf_op | source)
XLA Modules:
  0.0 76.2 jit_solution(12292081173602082792)
XLA Ops:
  0.0 1.2 %shard_map.74 = (f32[2,128,512]{2,1,0:T(8,128)S(1)}, f32[2,128,512]{2,1,0:T(8,128)S(1)}) custom-call(f32[2,512,512]{2,1,0:T(8,128)} %own.5), custom_call_target="tpu_custom_call" | custom-call | tf_op jit(solution)/shard_map/pallas_call | solution.py:322
  1.2 4.1 %collective-permute-start.1 = (f32[2,128,512]{2,1,0:T(8,128)S(1)}, f32[2,128,512]{2,1,0:T(8,128)S(1)}, u32[]{:S(2)}, u32[]{:S(2)}) collective-permute-start(f32[2,128,512]{2,1,0:T(8,128)S(1)} %get-tuple-element.27), channel_id=1, source_target_pairs={{0,1},{1,2},{2,3},{4,5},{5,6},{6,7},{8,9},{9,10},{10,11},{12,13},{... | collective-permute-start | bytes 1572872 | tf_op jit(solution)/shard_map/ppermute | solution.py:323
  5.3 1.3 %collective-permute-start.2 = (f32[2,128,512]{2,1,0:T(8,128)S(1)}, f32[2,128,512]{2,1,0:T(8,128)S(1)}, u32[]{:S(2)}, u32[]{:S(2)}) collective-permute-start(f32[2,128,512]{2,1,0:T(8,128)S(1)} %get-tuple-element.28), channel_id=1, source_target_pairs={{1,0},{2,1},{3,2},{5,4},{6,5},{7,6},{9,8},{10,9},{11,10},{13,12},{... | collective-permute-start | bytes 1572872 | tf_op jit(solution)/shard_map/ppermute | solution.py:324
  7.2 0.8 %copy.13 = s32[1,1,4,2]{3,2,1,0:T(4,128)S(1)} copy(s32[1,1,4,2]{2,3,1,0:T(2,128)} %param.9) | data formatting | bytes 64 | tf_op args[2]
  8.0 0.1 reshape.14
  8.1 0.1 add_bitcast_fusion.info
  8.2 1.8 %shard_map.73 = (f32[2,512,128]{2,1,0:T(8,128)S(1)}, f32[2,512,128]{2,1,0:T(8,128)S(1)}) custom-call(s32[1,10]{1,0:T(1,128)S(1)} %add_bitcast_fusion.info, f32[2,512,512]{2,1,0:T(8,128)} %own.5), custom_call_target="tpu_custom_call" | custom-call | tf_op jit(solution)/shard_map/pallas_call | solution.py:326
  10.0 1.0 %collective-permute-start.4 = (f32[2,512,128]{2,1,0:T(8,128)S(1)}, f32[2,512,128]{2,1,0:T(8,128)S(1)}, u32[]{:S(2)}, u32[]{:S(2)}) collective-permute-start(f32[2,512,128]{2,1,0:T(8,128)S(1)} %get-tuple-element.34), channel_id=1, source_target_pairs={{0,4},{4,0},{8,12},{12,8},{16,20},{20,16},{24,28},{28,24},{1,5},{5... | collective-permute-start | bytes 1572872 | tf_op jit(solution)/shard_map/ppermute | solution.py:327
  11.0 4.9 %collective-permute-done.1.up = f32[2,128,512]{2,1,0:T(8,128)S(1)} collective-permute-done((f32[2,128,512]{2,1,0:T(8,128)S(1)}, f32[2,128,512]{2,1,0:T(8,128)S(1)}, u32[]{:S(2)}, u32[]{:S(2)}) %collective-permute-start.1) | collective-permute-done | bytes 524320 | tf_op jit(solution)/shard_map/ppermute | solution.py:323
  15.8 3.9 %collective-permute-done.2.down = f32[2,128,512]{2,1,0:T(8,128)S(1)} collective-permute-done((f32[2,128,512]{2,1,0:T(8,128)S(1)}, f32[2,128,512]{2,1,0:T(8,128)S(1)}, u32[]{:S(2)}, u32[]{:S(2)}) %collective-permute-start.2) | collective-permute-done | bytes 524320 | tf_op jit(solution)/shard_map/ppermute | solution.py:324
  19.7 0.6 shard_map.75
  20.3 1.9 %collective-permute-start.5 = (f32[2,2,128,128]{3,2,1,0:T(8,128)S(1)}, f32[2,2,128,128]{3,2,1,0:T(8,128)S(1)}, u32[]{:S(2)}, u32[]{:S(2)}) collective-permute-start(f32[2,2,128,128]{3,2,1,0:T(8,128)S(1)} %get-tuple-element.35), channel_id=1, source_target_pairs={{0,4},{4,0},{8,12},{12,8},{16,20},{20,16},{24,28},{28,24},{1,5},{5... | collective-permute-start | bytes 786440 | tf_op jit(solution)/shard_map/ppermute | solution.py:345
  22.2 3.0 %collective-permute-start = (f32[2,512,128]{2,1,0:T(8,128)S(1)}, f32[2,512,128]{2,1,0:T(8,128)S(1)}, u32[]{:S(2)}, u32[]{:S(2)}) collective-permute-start(f32[2,512,128]{2,1,0:T(8,128)S(1)} %get-tuple-element.26), channel_id=1, source_target_pairs={{4,8},{12,16},{20,24},{8,4},{16,12},{24,20},{5,9},{13,17},{21,25},... | collective-permute-start | bytes 1572872 | tf_op jit(solution)/shard_map/ppermute | solution.py:328
  25.2 3.7 %shard_map.76 = (f32[4,256,256]{2,1,0:T(8,128)S(1)}, f32[2,6,768,128]{3,2,1,0:T(8,128)S(1)}, f32[2,6,768,128]{3,2,1,0:T(8,128)S(1)}, f32[3,2,256,256]{3,2,1,0:T(...) custom-call(f32[4,256,256]{2,1,0:T(8,128)} %bitcast.6, f32[2,512,512]{2,1,0:T(8,128)} %own.5, ...), custom_call_target="tpu_custom_call" | custom-call | flops 1000000000 | bytes 10000000 | tf_op jit(solution)/shard_map/pallas_call | solution.py:331
  29.0 2.5 %collective-permute-start.3 = (f32[2,2,128,128]{3,2,1,0:T(8,128)S(1)}, f32[2,2,128,128]{3,2,1,0:T(8,128)S(1)}, u32[]{:S(2)}, u32[]{:S(2)}) collective-permute-start(f32[2,2,128,128]{3,2,1,0:T(8,128)S(1)} %get-tuple-element.29), channel_id=1, source_target_pairs={{4,8},{12,16},{20,24},{8,4},{16,12},{24,20},{5,9},{13,17},{21,25},... | collective-permute-start | bytes 786440 | tf_op jit(solution)/shard_map/ppermute | solution.py:346
  31.5 0.0 collective-permute-done.4.in_e
  31.5 0.0 collective-permute-done.5.c_e
  31.5 8.2 %shard_map.77 = (f32[2,6,768,128]{3,2,1,0:T(8,128)S(1)}, f32[2,6,768,128]{3,2,1,0:T(8,128)S(1)}) custom-call(s32[1,10]{1,0:T(1,128)S(1)} %add_bitcast_fusion.info, f32[2,128,512]{2,1,0:T(8,128)S(1)} %collective-permute-done.1.up, f32[2,128,512]{2,1,0:T(8,128)S(1)} %collective-permute-done.2.down, ...), custom_call_target="tpu_custom_call", output_to_operand_aliasing={{0}: (9, {}), {1}: (10, {})} | custom-call | flops 10000000000 | bytes 10000000 | tf_op jit(solution)/shard_map/pallas_call | solution.py:360
  39.7 0.0 collective-permute-done.in_o
  39.7 3.9 %collective-permute-done.3.c_o = f32[2,2,128,128]{3,2,1,0:T(8,128)S(1)} collective-permute-done((f32[2,2,128,128]{3,2,1,0:T(8,128)S(1)}, f32[2,2,128,128]{3,2,1,0:T(8,128)S(1)}, u32[]{:S(2)}, u32[]{:S(2)}) %collective-permute-start.3) | collective-permute-done | bytes 262176 | tf_op jit(solution)/shard_map/ppermute | solution.py:346
  43.6 3.4 %shard_map.78 = (f32[2,6,768,128]{3,2,1,0:T(8,128)S(1)}, f32[2,6,768,128]{3,2,1,0:T(8,128)S(1)}, f32[2,768,128]{2,1,0:T(8,128)S(1)}, f32[2,512,128]{2,1,0:T(8,12...) custom-call(s32[1,10]{1,0:T(1,128)S(1)} %add_bitcast_fusion.info, ...), custom_call_target="tpu_custom_call", output_to_operand_aliasing={{0}: (7, {}), {1}: (8, {})} | custom-call | flops 10000000000 | bytes 10000000 | tf_op jit(solution)/shard_map/pallas_call | solution.py:372
  47.0 0.1 collective-permute-start.6
  47.1 4.1 %collective-permute-start.7 = (f32[2,512,128]{2,1,0:T(8,128)S(1)}, f32[2,512,128]{2,1,0:T(8,128)S(1)}, u32[]{:S(2)}, u32[]{:S(2)}) collective-permute-start(f32[2,512,128]{2,1,0:T(8,128)S(1)} %get-tuple-element.42), channel_id=1, source_target_pairs={{4,8},{12,16},{20,24},{8,4},{16,12},{24,20},{5,9},{13,17},{21,25},... | collective-permute-start | bytes 1572872 | tf_op jit(solution)/shard_map/ppermute | solution.py:385
  51.2 0.0 collective-permute-done.6.in_e
  51.2 0.6 shard_map.79
  51.8 3.2 %collective-permute-start.8 = (f32[2,4,128,128]{3,2,1,0:T(8,128)S(1)}, f32[2,4,128,128]{3,2,1,0:T(8,128)S(1)}, u32[]{:S(2)}, u32[]{:S(2)}) collective-permute-start(f32[2,4,128,128]{3,2,1,0:T(8,128)S(1)} %get-tuple-element.43), channel_id=1, source_target_pairs={{0,1},{1,2},{2,3},{4,5},{5,6},{6,7},{8,9},{9,10},{10,11},{12,13},{... | collective-permute-start | bytes 1572872 | tf_op jit(solution)/shard_map/ppermute | solution.py:389
  55.1 1.3 %collective-permute-start.9 = (f32[2,4,128,128]{3,2,1,0:T(8,128)S(1)}, f32[2,4,128,128]{3,2,1,0:T(8,128)S(1)}, u32[]{:S(2)}, u32[]{:S(2)}) collective-permute-start(f32[2,4,128,128]{3,2,1,0:T(8,128)S(1)} %get-tuple-element.44), channel_id=1, source_target_pairs={{1,0},{2,1},{3,2},{5,4},{6,5},{7,6},{9,8},{10,9},{11,10},{13,12},{... | collective-permute-start | bytes 1572872 | tf_op jit(solution)/shard_map/ppermute | solution.py:388
  56.4 4.6 %collective-permute-start.10 = (f32[2,128,128]{2,1,0:T(8,128)S(1)}, f32[2,128,128]{2,1,0:T(8,128)S(1)}, u32[]{:S(2)}, u32[]{:S(2)}) collective-permute-start(f32[2,128,128]{2,1,0:T(8,128)S(1)} %get-tuple-element.45), channel_id=1, source_target_pairs={{4,9},{12,17},{20,25},{8,5},{16,13},{24,21},{5,10},{13,18},{21,26}... | collective-permute-start | bytes 393224 | tf_op jit(solution)/shard_map/ppermute | solution.py:391
  61.0 1.3 %collective-permute-start.11 = (f32[2,128,128]{2,1,0:T(8,128)S(1)}, f32[2,128,128]{2,1,0:T(8,128)S(1)}, u32[]{:S(2)}, u32[]{:S(2)}) collective-permute-start(f32[2,128,128]{2,1,0:T(8,128)S(1)} %get-tuple-element.46), channel_id=1, source_target_pairs={{5,8},{13,16},{21,24},{9,4},{17,12},{25,20},{6,9},{14,17},{22,25},... | collective-permute-start | bytes 393224 | tf_op jit(solution)/shard_map/ppermute | solution.py:390
  62.3 4.6 %collective-permute-done.10.c_above = f32[2,128,128]{2,1,0:T(8,128)S(1)} collective-permute-done((f32[2,128,128]{2,1,0:T(8,128)S(1)}, f32[2,128,128]{2,1,0:T(8,128)S(1)}, u32[]{:S(2)}, u32[]{:S(2)}) %collective-permute-start.10) | collective-permute-done | bytes 131104 | tf_op jit(solution)/shard_map/ppermute | solution.py:391
  66.9 7.0 %collective-permute-done.11.c_below = f32[2,128,128]{2,1,0:T(8,128)S(1)} collective-permute-done((f32[2,128,128]{2,1,0:T(8,128)S(1)}, f32[2,128,128]{2,1,0:T(8,128)S(1)}, u32[]{:S(2)}, u32[]{:S(2)}) %collective-permute-start.11) | collective-permute-done | bytes 131104 | tf_op jit(solution)/shard_map/ppermute | solution.py:390
  74.0 0.0 collective-permute-done.7.in_o
  74.0 0.0 collective-permute-done.8.from_above
  74.0 0.0 collective-permute-done.9.from_below
  74.0 2.2 %shard_map.80 = f32[2,512,512]{2,1,0:T(8,128)} custom-call(s32[1,10]{1,0:T(1,128)S(1)} %add_bitcast_fusion.info, f32[2,6,768,128]{3,2,1,0:T(8,128)S(1)} %get-tuple-element.40.acc, f32[2,768,128]{2,1,0:T(8,128)S(1)} %collective-permute-done.6.in_e, f32[2,512,128]{2,1,0:T(8,128)S(1)} %collective-permute-done.7.in_o, ...), custom_call_target="tpu_custom_call" | custom-call | tf_op jit(solution)/shard_map/pallas_call | solution.py:392
Async XLA Ops:
  1.2 14.6 %collective-permute-start.1 = (f32[2,128,512]{2,1,0:T(8,128)S(1)}, f32[2,128,512]{2,1,0:T(8,128)S(1)}, u32[]{:S(2)}, u32[]{:S(2)}) collective-permute-start(f32[2,128,512]{2,1,0:T(8,128)S(1)} %get-tuple-element.27), channel_id=1, source_target_pairs={{0,1},{1,2},{2,3},{4,5},{5,6},{6,7},{8,9},{9,10},{10,11},{12,13},{... | collective-permute-start | bytes 1572872 | tf_op jit(solution)/shard_map/ppermute | solution.py:323
  5.3 14.4 %collective-permute-start.2 = (f32[2,128,512]{2,1,0:T(8,128)S(1)}, f32[2,128,512]{2,1,0:T(8,128)S(1)}, u32[]{:S(2)}, u32[]{:S(2)}) collective-permute-start(f32[2,128,512]{2,1,0:T(8,128)S(1)} %get-tuple-element.28), channel_id=1, source_target_pairs={{1,0},{2,1},{3,2},{5,4},{6,5},{7,6},{9,8},{10,9},{11,10},{13,12},{... | collective-permute-start | bytes 1572872 | tf_op jit(solution)/shard_map/ppermute | solution.py:324
  10.0 21.6 %collective-permute-start.4 = (f32[2,512,128]{2,1,0:T(8,128)S(1)}, f32[2,512,128]{2,1,0:T(8,128)S(1)}, u32[]{:S(2)}, u32[]{:S(2)}) collective-permute-start(f32[2,512,128]{2,1,0:T(8,128)S(1)} %get-tuple-element.34), channel_id=1, source_target_pairs={{0,4},{4,0},{8,12},{12,8},{16,20},{20,16},{24,28},{28,24},{1,5},{5... | collective-permute-start | bytes 1572872 | tf_op jit(solution)/shard_map/ppermute | solution.py:327
  20.3 11.2 %collective-permute-start.5 = (f32[2,2,128,128]{3,2,1,0:T(8,128)S(1)}, f32[2,2,128,128]{3,2,1,0:T(8,128)S(1)}, u32[]{:S(2)}, u32[]{:S(2)}) collective-permute-start(f32[2,2,128,128]{3,2,1,0:T(8,128)S(1)} %get-tuple-element.35), channel_id=1, source_target_pairs={{0,4},{4,0},{8,12},{12,8},{16,20},{20,16},{24,28},{28,24},{1,5},{5... | collective-permute-start | bytes 786440 | tf_op jit(solution)/shard_map/ppermute | solution.py:345
  22.2 17.5 %collective-permute-start = (f32[2,512,128]{2,1,0:T(8,128)S(1)}, f32[2,512,128]{2,1,0:T(8,128)S(1)}, u32[]{:S(2)}, u32[]{:S(2)}) collective-permute-start(f32[2,512,128]{2,1,0:T(8,128)S(1)} %get-tuple-element.26), channel_id=1, source_target_pairs={{4,8},{12,16},{20,24},{8,4},{16,12},{24,20},{5,9},{13,17},{21,25},... | collective-permute-start | bytes 1572872 | tf_op jit(solution)/shard_map/ppermute | solution.py:328
  29.0 14.7 %collective-permute-start.3 = (f32[2,2,128,128]{3,2,1,0:T(8,128)S(1)}, f32[2,2,128,128]{3,2,1,0:T(8,128)S(1)}, u32[]{:S(2)}, u32[]{:S(2)}) collective-permute-start(f32[2,2,128,128]{3,2,1,0:T(8,128)S(1)} %get-tuple-element.29), channel_id=1, source_target_pairs={{4,8},{12,16},{20,24},{8,4},{16,12},{24,20},{5,9},{13,17},{21,25},... | collective-permute-start | bytes 786440 | tf_op jit(solution)/shard_map/ppermute | solution.py:346
  47.0 4.2 %collective-permute-start.6 = (f32[2,768,128]{2,1,0:T(8,128)S(1)}, f32[2,768,128]{2,1,0:T(8,128)S(1)}, u32[]{:S(2)}, u32[]{:S(2)}) collective-permute-start(f32[2,768,128]{2,1,0:T(8,128)S(1)} %get-tuple-element.41), channel_id=1, source_target_pairs={{0,4},{4,0},{8,12},{12,8},{16,20},{20,16},{24,28},{28,24},{1,5},{5... | collective-permute-start | bytes 2359304 | tf_op jit(solution)/shard_map/ppermute | solution.py:384
  47.1 26.9 %collective-permute-start.7 = (f32[2,512,128]{2,1,0:T(8,128)S(1)}, f32[2,512,128]{2,1,0:T(8,128)S(1)}, u32[]{:S(2)}, u32[]{:S(2)}) collective-permute-start(f32[2,512,128]{2,1,0:T(8,128)S(1)} %get-tuple-element.42), channel_id=1, source_target_pairs={{4,8},{12,16},{20,24},{8,4},{16,12},{24,20},{5,9},{13,17},{21,25},... | collective-permute-start | bytes 1572872 | tf_op jit(solution)/shard_map/ppermute | solution.py:385
  51.8 22.1 %collective-permute-start.8 = (f32[2,4,128,128]{3,2,1,0:T(8,128)S(1)}, f32[2,4,128,128]{3,2,1,0:T(8,128)S(1)}, u32[]{:S(2)}, u32[]{:S(2)}) collective-permute-start(f32[2,4,128,128]{3,2,1,0:T(8,128)S(1)} %get-tuple-element.43), channel_id=1, source_target_pairs={{0,1},{1,2},{2,3},{4,5},{5,6},{6,7},{8,9},{9,10},{10,11},{12,13},{... | collective-permute-start | bytes 1572872 | tf_op jit(solution)/shard_map/ppermute | solution.py:389
  55.1 18.9 %collective-permute-start.9 = (f32[2,4,128,128]{3,2,1,0:T(8,128)S(1)}, f32[2,4,128,128]{3,2,1,0:T(8,128)S(1)}, u32[]{:S(2)}, u32[]{:S(2)}) collective-permute-start(f32[2,4,128,128]{3,2,1,0:T(8,128)S(1)} %get-tuple-element.44), channel_id=1, source_target_pairs={{1,0},{2,1},{3,2},{5,4},{6,5},{7,6},{9,8},{10,9},{11,10},{13,12},{... | collective-permute-start | bytes 1572872 | tf_op jit(solution)/shard_map/ppermute | solution.py:388
  56.4 10.5 %collective-permute-start.10 = (f32[2,128,128]{2,1,0:T(8,128)S(1)}, f32[2,128,128]{2,1,0:T(8,128)S(1)}, u32[]{:S(2)}, u32[]{:S(2)}) collective-permute-start(f32[2,128,128]{2,1,0:T(8,128)S(1)} %get-tuple-element.45), channel_id=1, source_target_pairs={{4,9},{12,17},{20,25},{8,5},{16,13},{24,21},{5,10},{13,18},{21,26}... | collective-permute-start | bytes 393224 | tf_op jit(solution)/shard_map/ppermute | solution.py:391
  61.0 12.9 %collective-permute-start.11 = (f32[2,128,128]{2,1,0:T(8,128)S(1)}, f32[2,128,128]{2,1,0:T(8,128)S(1)}, u32[]{:S(2)}, u32[]{:S(2)}) collective-permute-start(f32[2,128,128]{2,1,0:T(8,128)S(1)} %get-tuple-element.46), channel_id=1, source_target_pairs={{5,8},{13,16},{21,24},{9,4},{17,12},{25,20},{6,9},{14,17},{22,25},... | collective-permute-start | bytes 393224 | tf_op jit(solution)/shard_map/ppermute | solution.py:390
where the time goes:
time: 76.5 us; the launch traced here: 76.2 us
  starting transfers between devices  28.4 us (37%)
  waiting for transfers between devices  24.3 us (32%)
  Pallas kernels  21.7 us (28%)
  local copies, waits for them, and re-layouts  0.85 us (1%)
  between operations  0.83 us (1%)
    pallas_call x1, Pallas kernels, program(): call(near_kernel, [SM] + [ANY] * 4 + [VM] * 6, [VM] * 2, [shape(ext_shape...  8.17 us
    ppermute x1, waiting for transfers between devices, program(): c_below = lax.ppermute(rim_top, ('gx', 'gy'), diagonal(pairs_up))  7.03 us
    ppermute x1, waiting for transfers between devices, program(): up = lax.ppermute(to_down, 'gy', pairs_down)  4.87 us
    ppermute x1, starting transfers between devices, program(): c_above = lax.ppermute(rim_low, ('gx', 'gy'), diagonal(pairs_down))  4.61 us
    ppermute x1, waiting for transfers between devices, program(): c_above = lax.ppermute(rim_low, ('gx', 'gy'), diagonal(pairs_down))  4.61 us
    ppermute x1, starting transfers between devices, program(): back_o = lax.ppermute(rim_o, 'gx', pairs_o)  4.08 us
    ppermute x1, starting transfers between devices, program(): up = lax.ppermute(to_down, 'gy', pairs_down)  4.05 us
    ppermute x1, waiting for transfers between devices, program(): c_o = lax.ppermute(corner_o, 'gx', pairs_o)  3.93 us
  transfers between devices with their start and end apart: 12, of which 5 were waited for; matrix products, arithmetic and copies ran while one was open for 1% of the time, Pallas kernels for 20%

commit v1 on v0

v1 whole, which is shorter than its diff:
```python
import functools
import math

import jax
import jax.numpy as jnp
import numpy as np
from jax import lax
from jax.experimental import pallas as pl
from jax.experimental.pallas import tpu as pltpu
from jax.sharding import PartitionSpec as P


HALO = 128
LANE = 128
F32 = jnp.float32
BF16 = jnp.bfloat16
ANY = pl.BlockSpec(memory_space=pl.ANY)
VM = pl.BlockSpec(memory_space=pltpu.VMEM)
SM = pl.BlockSpec(memory_space=pltpu.SMEM)
HB = pl.BlockSpec(memory_space=pltpu.HBM)


def dft_tables(width):
    half = width // 2
    t = np.arange(width)
    order = np.concatenate([t[0::2], t[1::2]])
    phase = 2.0 * math.pi / width * np.mod(np.outer(t, order), width)
    c = np.cos(phase) / math.sqrt(width)
    s = np.sin(phase) / math.sqrt(width)
    blocks, small = [], []
    for b in (slice(0, half), slice(half, width)):
        blocks += [np.concatenate([c[:, b], s[:, b]]), np.concatenate([-s[:, b], c[:, b]])]
        ct, st = c[:half, b].T, s[:half, b].T
        small.append(np.block([[ct, st], [-st, ct]]))
    fwd = np.concatenate(blocks, axis=1)
    big = np.stack([fwd, fwd.T])
    small = np.stack(small + [m.T for m in small])
    return jnp.asarray(big, BF16), jnp.asarray(small, BF16)


def dot(a, b):
    return jnp.dot(a, b, preferred_element_type=F32)


def sides(blocks):
    odd = lax.rem(lax.axis_index("gx"), 2) == 1
    return jnp.where(odd, 0, blocks + 1), jnp.where(odd, blocks + 1, 0)


def ends(far):
    odd = lax.rem(lax.axis_index("gy"), 2) == 1
    first, second = jnp.where(odd, 0, far), jnp.where(odd, far, 0)
    return pl.multiple_of(first, HALO), pl.multiple_of(second, HALO)


def rows_kernel(own, first, second, sem):
    offsets = ends(own.shape[1] - HALO)
    copies = [
        pltpu.make_async_copy(own.at[:, pl.ds(at, HALO), :], strip, sem.at[i])
        for i, (at, strip) in enumerate(zip(offsets, (first, second)))
    ]
    for cp in copies:
        cp.start()
    for cp in copies:
        cp.wait()


def edge_kernel(which, own, edge, sem):
    block = sides(own.shape[2] // LANE - 2)[which]
    lanes = pl.ds(pl.multiple_of(block * LANE, LANE), LANE)
    cp = pltpu.make_async_copy(own.at[:, :, lanes], edge, sem.at[0])
    cp.start()
    cp.wait()


def inner_edge_kernel(*refs):
    edge_kernel(0, *refs)


def outer_edge_kernel(*refs):
    edge_kernel(1, *refs)


def corners_kernel(first, second, corner_e, corner_o):
    block_e, block_o = sides(first.shape[2] // LANE - 2)
    for i, strip in enumerate((first, second)):
        corner_e[i] = strip[:, :, pl.ds(pl.multiple_of(block_e * LANE, LANE), LANE)]
        corner_o[i] = strip[:, :, pl.ds(pl.multiple_of(block_o * LANE, LANE), LANE)]


def prepare_kernel(info, measured_h, own, probe, big, small, amp, ext, acc, probe_v, big_v, small_v, measured, sem):
    slots, width, _ = measured.shape
    half = width // 2
    rows = own.shape[1]
    blocks = own.shape[2] // LANE
    copies = [(measured_h, measured), (probe, probe_v), (big, big_v), (small, small_v)]
    for b in range(blocks):
        copies.append((own.at[:, :, pl.ds(b * LANE, LANE)], ext.at[:, b + 1, pl.ds(HALO, rows)]))
    copies = [pltpu.make_async_copy(p, q, sem.at[i]) for i, (p, q) in enumerate(copies)]
    for cp in copies:
        cp.start()
    acc[...] = jnp.zeros_like(acc)
    i = lax.broadcasted_iota(jnp.int32, (width, width), 0)
    j = lax.broadcasted_iota(jnp.int32, (width, width), 1)
    source = jnp.where(j < half, 2 * j, 2 * (j - half) + 1)
    cols = (i == source).astype(F32)
    source = jnp.where(i < half, 2 * i, 2 * (i - half) + 1)
    perm = (j == source).astype(F32)
    copies[0].wait()
    for k in range(slots):
        a = jnp.sqrt(measured[k])
        a = jnp.dot(perm, a, precision=lax.Precision.HIGHEST, preferred_element_type=F32)
        amp[k] = jnp.dot(a, cols, precision=lax.Precision.HIGHEST, preferred_element_type=F32)
    for cp in copies[1:]:
        cp.wait()


def one_frame(slot, info, ext, acc, probe, amp, big, small, patch, x, y, xa, xb, u, v, wave, factor):
    modes, _, width, _ = probe.shape
    h = width // 2
    chunk = 64
    lo, hi = slice(0, h), slice(h, width)
    r = info[0, 1 + 2 * slot]
    c = info[0, 2 + 2 * slot]
    q = jnp.minimum(c // LANE, ext.shape[1] - 3)
    s = c - q * LANE
    left = jnp.bitwise_and(LANE - s, LANE - 1)
    right = jnp.bitwise_and(s, LANE - 1)
    lane = lax.broadcasted_iota(jnp.int32, (chunk, LANE), 1)
    keep = lane < LANE - s
    for ch in range(2):
        for i in range(0, width, chunk):
            rows = pl.ds(r + i, chunk)
            rot = [pltpu.roll(ext[ch, q + t, rows, :], left, 1) for t in range(3)]
            patch[ch, i : i + chunk, lo] = jnp.where(keep, rot[0], rot[1])
            patch[ch, i : i + chunk, hi] = jnp.where(keep, rot[1], rot[2])
    for m in range(modes):
        for i in range(0, width, chunk):
            rows = slice(i, i + chunk)
            for cc in (lo, hi):
                pr, pi = probe[m, 0, rows, cc], probe[m, 1, rows, cc]
                o_re, o_im = patch[0, rows, cc], patch[1, rows, cc]
                x[m, rows, cc] = (pr * o_re - pi * o_im).astype(BF16)
                x[m, rows, slice(width + cc.start, width + cc.stop)] = (pr * o_im + pi * o_re).astype(BF16)
        for k in range(2):
            e = dot(x[m], big[0, :, k * width : (k + 1) * width])
            y[m, 0:width, k * h : (k + 1) * h] = e[:, lo].astype(BF16)
            y[m, width:, k * h : (k + 1) * h] = e[:, hi].astype(BF16)
    for m in range(modes):
        for k in range(2):
            p = dot(big[1, k * width : (k + 1) * width], y[m])
            wave[m, k] = p
            square = p[lo] * p[lo] + p[hi] * p[hi]
            factor[k] = square if m == 0 else factor[k] + square
    for k in range(2):
        factor[k] = 1.0 - amp[slot, k * h : (k + 1) * h, :] * lax.rsqrt(factor[k] + 1.0)
    for m in range(modes):
        for k in range(2):
            f = factor[k]
            for part in (lo, hi):
                w = f * wave[m, k, part, :]
                xa[m, k * h : (k + 1) * h, part] = w[:, lo].astype(BF16)
                xb[m, k * h : (k + 1) * h, part] = w[:, hi].astype(BF16)
    for m in range(modes):
        a, b = dot(xa[m], small[0]), dot(xb[m], small[1])
        for cc, z in ((lo, a + b), (hi, a - b)):
            for part in (lo, hi):
                u[m, part, cc] = z[lo, part].astype(BF16)
                v[m, part, cc] = z[hi, part].astype(BF16)
    for m in range(modes):
        a, b = dot(small[2], u[m]), dot(small[3], v[m])
        for rows, z in ((lo, a + b), (hi, a - b)):
            pr, pi = probe[m, 0, rows, :], probe[m, 1, rows, :]
            g_re = pr * z[lo] + pi * z[hi]
            g_im = pr * z[hi] - pi * z[lo]
            if m > 0:
                g_re = g_re + patch[0, rows, :]
                g_im = g_im + patch[1, rows, :]
            patch[0, rows, :] = g_re
            patch[1, rows, :] = g_im
    first = lane < s
    for ch in range(2):
        for i in range(0, width, chunk):
            rows = pl.ds(r + i, chunk)
            g0 = pltpu.roll(patch[ch, i : i + chunk, lo], right, 1)
            g1 = pltpu.roll(patch[ch, i : i + chunk, hi], right, 1)
            zero = jnp.zeros_like(g0)
            acc[ch, q, rows, :] += jnp.where(first, zero, g0)
            acc[ch, q + 1, rows, :] += jnp.where(first, g0, g1)
            acc[ch, q + 2, rows, :] += jnp.where(first, g1, zero)


def frame_stage(slot, info, cols, width):
    c = info[0, 2 + 2 * slot]
    odd = lax.rem(lax.axis_index("gx"), 2) == 1
    return jnp.where(odd, c > cols + HALO - width, c < HALO).astype(jnp.int32)


def run_frames(stage, info, ext, acc, probe, amp, big, small, *scratch):
    width = probe.shape[-1]
    cols = (ext.shape[1] - 2) * LANE

    def step(slot, carry):
        @pl.when(frame_stage(slot, info, cols, width) == stage)
        def _():
            one_frame(slot, info, ext, acc, probe, amp, big, small, *scratch)

        return carry

    lax.fori_loop(0, info[0, 0], step, 0)


def near_kernel(info, first, second, in_e, c_e, probe, amp, big, small, ext_in, acc_in, ext, acc, *rest):
    blocks = ext.shape[1] - 2
    rows = ext.shape[2] - 2 * HALO
    col_e, _ = sides(blocks)
    for i, (at, strip) in enumerate(zip(ends(HALO + rows), (first, second))):
        for ch in range(2):
            for b in range(blocks):
                ext[ch, b + 1, pl.ds(at, HALO)] = strip[ch, :, b * LANE : (b + 1) * LANE]
            ext[ch, col_e, pl.ds(at, HALO)] = c_e[i, ch]
    for ch in range(2):
        ext[ch, col_e, HALO : HALO + rows] = in_e[ch]
    run_frames(0, info, ext, acc, probe, amp, big, small, *rest)


def outer_kernel(info, in_o, c_o, probe, amp, big, small, ext_in, acc_in,
                 ext, acc, rim_e, rim_o, rim_first, rim_second, *rest):
    blocks = ext.shape[1] - 2
    rows = ext.shape[2] - 2 * HALO
    col_e, col_o = sides(blocks)
    offsets = ends(HALO + rows)
    for ch in range(2):
        for i, at in enumerate(offsets):
            ext[ch, col_o, pl.ds(at, HALO)] = c_o[i, ch]
        ext[ch, col_o, HALO : HALO + rows] = in_o[ch]
    run_frames(1, info, ext, acc, probe, amp, big, small, *rest)
    for ch in range(2):
        rim_e[ch] = acc[ch, col_e]
        for at, rim in zip(offsets, (rim_first, rim_second)):
            rim[ch] = acc[ch, col_o, pl.ds(at, HALO)]
        rim_o[ch] = acc[ch, col_o, HALO : HALO + rows]


def rims_kernel(acc, in_e, first, second):
    blocks = acc.shape[1] - 2
    block_e, _ = sides(blocks - 2)
    for at, strip in zip(ends(acc.shape[2] - HALO), (first, second)):
        for ch in range(2):
            for b in range(blocks):
                strip[ch, b] = acc[ch, b + 1, pl.ds(at, HALO)]
            strip[ch, block_e] += in_e[ch, pl.ds(at, HALO)]


def inner_join_kernel(acc, in_e, first, second, out, buf, sem):
    blocks = acc.shape[1] - 2
    rows = acc.shape[2] - 2 * HALO
    block_e, block_o = sides(blocks - 2)
    start = jnp.where(block_o == 0, 1, 0)
    copies = []
    for t in range(blocks - 1):
        b = start + t
        for ch in range(2):
            buf[ch, t] = acc[ch, b + 1, HALO : HALO + rows, :]
            for at, strip in zip(ends(rows - HALO), (first, second)):
                buf[ch, t, pl.ds(at, HALO)] += strip[ch, b]
    for ch in range(2):
        buf[ch, block_e - start] += in_e[ch, HALO : HALO + rows]
    for t in range(blocks - 1):
        lanes = pl.ds(pl.multiple_of((start + t) * LANE, LANE), LANE)
        copies.append(pltpu.make_async_copy(buf.at[:, t], out.at[:, :, lanes], sem.at[t]))
        copies[-1].start()
    for cp in copies:
        cp.wait()


def outer_join_kernel(acc, in_o, first, second, c_first, c_second, out_in, out, buf, sem):
    blocks = acc.shape[1] - 2
    rows = acc.shape[2] - 2 * HALO
    _, b = sides(blocks - 2)
    for ch in range(2):
        buf[ch] = acc[ch, b + 1, HALO : HALO + rows, :] + in_o[ch]
        for at, strip, corner in zip(ends(rows - HALO), (first, second), (c_first, c_second)):
            buf[ch, pl.ds(at, HALO)] += strip[ch, b] + corner[ch]
    lanes = pl.ds(pl.multiple_of(b * LANE, LANE), LANE)
    cp = pltpu.make_async_copy(buf, out.at[:, :, lanes], sem.at[0])
    cp.start()
    cp.wait()


def call(kernel, in_specs, out_specs, out_shape, scratch=(), limit=8 << 20, flops=0, moved=0, aliases=None):
    return pl.pallas_call(
        kernel,
        in_specs=in_specs,
        out_specs=out_specs,
        out_shape=out_shape,
        scratch_shapes=scratch,
        input_output_aliases=aliases or {},
        compiler_params=pltpu.CompilerParams(vmem_limit_bytes=limit),
        cost_estimate=pl.CostEstimate(flops=flops, bytes_accessed=moved, transcendentals=0),
    )


def shift(array, axis, pairs):
    return lax.ppermute(array, axis, pairs)


def program(object_field, probe, positions, frame_count, measured):
    width = probe.shape[-1]
    modes = probe.shape[0]
    _, rows, cols = object_field.shape
    blocks = cols // LANE
    n_gx = lax.axis_size("gx")
    n_gy = lax.axis_size("gy")
    slots = measured.shape[2]
    info = jnp.concatenate([frame_count.reshape(1), positions.reshape(2 * slots)]).reshape(1, -1)
    object_field, probe, measured = [pltpu.with_memory_space_constraint(a, pltpu.HBM) for a in (object_field, probe, measured[0, 0])]
    pairs_e = [(i, i ^ 1) for i in range(n_gx) if i ^ 1 < n_gx]
    pairs_o = [(i, i + 1) for i in range(1, n_gx - 1, 2)]
    pairs_o += [(j, i) for i, j in pairs_o]
    pairs_1 = [(i, i ^ 1) for i in range(n_gy) if i ^ 1 < n_gy]
    pairs_2 = [(i, i + 1) for i in range(1, n_gy - 1, 2)]
    pairs_2 += [(j, i) for i, j in pairs_2]

    def diagonal(pairs):
        return [(i * n_gy + z, j * n_gy + w) for z, w in pairs for i, j in pairs_o]

    shape = functools.partial(jax.ShapeDtypeStruct, dtype=F32)
    vmem = pltpu.VMEM
    dma = pltpu.SemaphoreType.DMA
    big, small = [pltpu.with_memory_space_constraint(a, pltpu.HBM) for a in dft_tables(width)]

    strip = shape((2, HALO, cols))
    edge = shape((2, rows, HALO))
    first, second = call(rows_kernel, [HB], [VM] * 2, [strip] * 2, [dma((2,))])(object_field)
    first = shift(first, "gy", pairs_1)
    second = shift(second, "gy", pairs_2)
    in_o = shift(call(outer_edge_kernel, [HB], VM, edge, [dma((1,))])(object_field), "gx", pairs_o)
    in_e = shift(call(inner_edge_kernel, [HB], VM, edge, [dma((1,))])(object_field), "gx", pairs_e)

    ext_shape = (2, blocks + 2, rows + 2 * HALO, LANE)
    amp, ext, acc, probe, big, small = call(
        prepare_kernel,
        [SM] + [HB] * 5,
        [VM] * 6,
        [shape(measured.shape), shape(ext_shape), shape(ext_shape), shape(probe.shape),
         jax.ShapeDtypeStruct(big.shape, BF16), jax.ShapeDtypeStruct(small.shape, BF16)],
        [vmem(measured.shape, F32), dma((4 + blocks,))],
        limit=24 << 20,
        flops=10**9,
        moved=10**7,
    )(info, measured, object_field, probe, big, small)

    corner = shape((2, 2, HALO, HALO))
    corner_e, corner_o = call(corners_kernel, [VM] * 2, [VM] * 2, [corner] * 2)(first, second)
    c_e = shift(corner_e, "gx", pairs_e)
    c_o = shift(corner_o, "gx", pairs_o)

    work = [
        vmem((2, width, width), F32),
        vmem((modes, width, 2 * width), BF16),
        vmem((modes, 2 * width, width), BF16),
        vmem((modes, width, width), BF16),
        vmem((modes, width, width), BF16),
        vmem((modes, width, width), BF16),
        vmem((modes, width, width), BF16),
        vmem((modes, 2, width, width), F32),
        vmem((2, width // 2, width), F32),
    ]
    ext, acc = call(
        near_kernel,
        [SM] + [VM] * 10,
        [VM] * 2,
        [shape(ext_shape)] * 2,
        work,
        limit=32 << 20,
        flops=10**10,
        moved=10**7,
        aliases={9: 0, 10: 1},
    )(info, first, second, in_e, c_e, probe, amp, big, small, ext, acc)
    piece = shape((2, HALO, HALO))
    _, acc, rim_e, rim_o, rim_1, rim_2 = call(
        outer_kernel,
        [SM] + [VM] * 8,
        [VM] * 6,
        [shape(ext_shape)] * 2 + [shape((2, rows + 2 * HALO, HALO)), edge, piece, piece],
        work,
        limit=32 << 20,
        flops=10**10,
        moved=10**7,
        aliases={7: 0, 8: 1},
    )(info, in_o, c_o, probe, amp, big, small, ext, acc)

    back_e = shift(rim_e, "gx", pairs_e)
    back_o = shift(rim_o, "gx", pairs_o)
    strip = shape((2, blocks, HALO, LANE))
    first, second = call(rims_kernel, [VM] * 2, [VM] * 2, [strip] * 2)(acc, back_e)
    first = shift(first, "gy", pairs_1)
    second = shift(second, "gy", pairs_2)
    c_first = shift(rim_1, ("gx", "gy"), diagonal(pairs_1))
    c_second = shift(rim_2, ("gx", "gy"), diagonal(pairs_2))
    whole = shape(object_field.shape)
    out = call(
        inner_join_kernel,
        [VM] * 4,
        HB,
        whole,
        [vmem((2, blocks - 1, rows, LANE), F32), dma((blocks - 1,))],
    )(acc, back_e, first, second)
    return call(
        outer_join_kernel,
        [VM] * 6 + [HB],
        HB,
        whole,
        [vmem((2, rows, LANE), F32), dma((1,))],
        aliases={6: 0},
    )(acc, back_o, first, second, c_first, c_second, out)


def solution(mesh):
    return jax.shard_map(
        program,
        mesh=mesh,
        in_specs=(
            P(None, "gy", "gx"),
            P(),
            P("gy", "gx", None, None),
            P("gy", "gx"),
            P("gy", "gx", None, None, None),
        ),
        out_specs=P(None, "gy", "gx"),
        check_vma=False,
    )
```

time: 76.5 us -> 74 us (0.967)
  the two profiles are of different devices: /device:TPU:1 before, /device:TPU:11 now
where the time goes in v1:
time: 74 us; the launch traced here: 73.3 us
  starting transfers between devices  27.4 us (37%)
  waiting for transfers between devices  22.5 us (30%)
  Pallas kernels  22.3 us (30%)
  between operations  0.82 us (1%)
    ppermute x12, starting transfers between devices, shift(): return lax.ppermute(array, axis, pairs)  27.4 us
    ppermute x12, waiting for transfers between devices, shift(): return lax.ppermute(array, axis, pairs)  22.5 us
    pallas_call x1, Pallas kernels, program(): call(near_kernel, [SM] + [VM] * 10, [VM] * 2, [shape(ext_shape)] * 2, wor...  8.36 us
    pallas_call x1, Pallas kernels, program(): call(prepare_kernel, [SM] + [HB] * 5, [VM] * 6, [shape(measured.shape), s...  4.26 us
    pallas_call x1, Pallas kernels, program(): call(outer_kernel, [SM] + [VM] * 8, [VM] * 6, [shape(ext_shape)] * 2 + [s...  3.17 us
  transfers between devices with their start and end apart: 12, of which 8 were waited for; matrix products, arithmetic and copies ran while one was open for 0% of the time, Pallas kernels for 23%

profile of v1, /device:TPU:11, one launch (start us, length us, event | category | flops | bytes accessed | tf_op | source)
XLA Modules:
  0.0 73.3 jit_solution(11136472109254744694)
XLA Ops:
  0.0 0.0 copy-start
  0.0 1.2 %shard_map.74 = (f32[2,128,512]{2,1,0:T(8,128)S(1)}, f32[2,128,512]{2,1,0:T(8,128)S(1)}) custom-call(f32[2,512,512]{2,1,0:T(8,128)} %refs_0_.3), custom_call_target="tpu_custom_call" | custom-call | tf_op jit(solution)/shard_map/pallas_call | solution.py:335
  1.2 0.2 collective-permute-start.1
  1.5 4.3 %collective-permute-start.2 = (f32[2,128,512]{2,1,0:T(8,128)S(1)}, f32[2,128,512]{2,1,0:T(8,128)S(1)}, u32[]{:S(2)}, u32[]{:S(2)}) collective-permute-start(f32[2,128,512]{2,1,0:T(8,128)S(1)} %get-tuple-element.25), channel_id=1, source_target_pairs={{1,2},{2,1},{5,6},{6,5},{9,10},{10,9},{13,14},{14,13},{17,18},{18,... | collective-permute-start | bytes 1572872 | tf_op jit(solution)/shard_map/ppermute | solution.py:305
  5.8 1.1 %shard_map.77 = f32[2,512,128]{2,1,0:T(8,128)S(1)} custom-call(f32[2,512,512]{2,1,0:T(8,128)} %refs_0_.3), custom_call_target="tpu_custom_call" | custom-call | tf_op jit(solution)/shard_map/pallas_call | solution.py:339
  6.9 1.3 %collective-permute-start.4 = (f32[2,512,128]{2,1,0:T(8,128)S(1)}, f32[2,512,128]{2,1,0:T(8,128)S(1)}, u32[]{:S(2)}, u32[]{:S(2)}) collective-permute-start(f32[2,512,128]{2,1,0:T(8,128)S(1)} %shard_map.77), channel_id=1, source_target_pairs={{0,4},{4,0},{8,12},{12,8},{16,20},{20,16},{24,28},{28,24},{1,5},{5... | collective-permute-start | bytes 1572872 | tf_op jit(solution)/shard_map/ppermute | solution.py:305
  8.2 5.9 %collective-permute-done.1.first = f32[2,128,512]{2,1,0:T(8,128)S(1)} collective-permute-done((f32[2,128,512]{2,1,0:T(8,128)S(1)}, f32[2,128,512]{2,1,0:T(8,128)S(1)}, u32[]{:S(2)}, u32[]{:S(2)}) %collective-permute-start.1) | collective-permute-done | bytes 524320 | tf_op jit(solution)/shard_map/ppermute | solution.py:305
  14.1 3.0 %collective-permute-done.2.second = f32[2,128,512]{2,1,0:T(8,128)S(1)} collective-permute-done((f32[2,128,512]{2,1,0:T(8,128)S(1)}, f32[2,128,512]{2,1,0:T(8,128)S(1)}, u32[]{:S(2)}, u32[]{:S(2)}) %collective-permute-start.2) | collective-permute-done | bytes 524320 | tf_op jit(solution)/shard_map/ppermute | solution.py:305
  17.1 0.8 %shard_map.75 = (f32[2,2,128,128]{3,2,1,0:T(8,128)}, f32[2,2,128,128]{3,2,1,0:T(8,128)S(1)}) custom-call(f32[2,128,512]{2,1,0:T(8,128)S(1)} %collective-permute-done.1.first, f32[2,128,512]{2,1,0:T(8,128)S(1)} %collective-permute-done.2.second), custom_call_target="tpu_custom_call" | custom-call | tf_op jit(solution)/shard_map/pallas_call | solution.py:355
  17.9 1.5 %collective-permute-start.5 = (f32[2,2,128,128]{3,2,1,0:T(8,128)}, f32[2,2,128,128]{3,2,1,0:T(8,128)}, u32[]{:S(2)}, u32[]{:S(2)}) collective-permute-start(f32[2,2,128,128]{3,2,1,0:T(8,128)} %get-tuple-element.31), channel_id=1, source_target_pairs={{0,4},{4,0},{8,12},{12,8},{16,20},{20,16},{24,28},{28,24},{1,5},{5... | collective-permute-start | bytes 786440 | tf_op jit(solution)/shard_map/ppermute | solution.py:305
  19.4 1.0 %shard_map.73 = f32[2,512,128]{2,1,0:T(8,128)S(1)} custom-call(f32[2,512,512]{2,1,0:T(8,128)} %refs_0_.3), custom_call_target="tpu_custom_call" | custom-call | tf_op jit(solution)/shard_map/pallas_call | solution.py:338
  20.5 3.0 %collective-permute-start = (f32[2,512,128]{2,1,0:T(8,128)S(1)}, f32[2,512,128]{2,1,0:T(8,128)S(1)}, u32[]{:S(2)}, u32[]{:S(2)}) collective-permute-start(f32[2,512,128]{2,1,0:T(8,128)S(1)} %shard_map.73), channel_id=1, source_target_pairs={{4,8},{12,16},{20,24},{8,4},{16,12},{24,20},{5,9},{13,17},{21,25},... | collective-permute-start | bytes 1572872 | tf_op jit(solution)/shard_map/ppermute | solution.py:305
  23.5 0.0 copy-done
  23.5 0.1 copy.14
  23.6 0.1 reshape.10
  24.4 0.1 add_bitcast_fusion.info
  24.4 4.3 %shard_map.76 = (f32[4,256,256]{2,1,0:T(8,128)S(1)}, f32[2,6,768,128]{3,2,1,0:T(8,128)S(1)}, f32[2,6,768,128]{3,2,1,0:T(8,128)S(1)}, f32[3,2,256,256]{3,2,1,0:T(...) custom-call(s32[1,9]{1,0:T(1,128)S(1)} %add_bitcast_fusion.info, f32[4,256,256]{2,1,0:T(8,128)} %bitcast.5, ...), custom_call_target="tpu_custom_call" | custom-call | flops 1000000000 | bytes 10000000 | tf_op jit(solution)/shard_map/pallas_call | solution.py:342
  28.7 3.5 %collective-permute-start.3 = (f32[2,2,128,128]{3,2,1,0:T(8,128)S(1)}, f32[2,2,128,128]{3,2,1,0:T(8,128)S(1)}, u32[]{:S(2)}, u32[]{:S(2)}) collective-permute-start(f32[2,2,128,128]{3,2,1,0:T(8,128)S(1)} %get-tuple-element.26), channel_id=1, source_target_pairs={{4,8},{12,16},{20,24},{8,4},{16,12},{24,20},{5,9},{13,17},{21,25},... | collective-permute-start | bytes 786440 | tf_op jit(solution)/shard_map/ppermute | solution.py:305
  32.2 0.0 collective-permute-done.4.in_e
  32.2 0.0 collective-permute-done.5.c_e
  32.2 8.4 %shard_map.78 = (f32[2,6,768,128]{3,2,1,0:T(8,128)S(1)}, f32[2,6,768,128]{3,2,1,0:T(8,128)S(1)}) custom-call(s32[1,9]{1,0:T(1,128)S(1)} %add_bitcast_fusion.info, f32[2,128,512]{2,1,0:T(8,128)S(1)} %collective-permute-done.1.first, f32[2,128,512]{2,1,0:T(8,128)S(1)} %collective-permute-done.2.second, ...), custom_call_target="tpu_custom_call", output_to_operand_aliasing={{0}: (9, {}), {1}: (10, {})} | custom-call | flops 10000000000 | bytes 10000000 | tf_op jit(solution)/shard_map/pallas_call | solution.py:370
  40.5 0.0 collective-permute-done.in_o
  40.6 1.9 %collective-permute-done.3.c_o = f32[2,2,128,128]{3,2,1,0:T(8,128)S(1)} collective-permute-done((f32[2,2,128,128]{3,2,1,0:T(8,128)S(1)}, f32[2,2,128,128]{3,2,1,0:T(8,128)S(1)}, u32[]{:S(2)}, u32[]{:S(2)}) %collective-permute-start.3) | collective-permute-done | bytes 262176 | tf_op jit(solution)/shard_map/ppermute | solution.py:305
  42.5 3.2 %shard_map.79 = (f32[2,6,768,128]{3,2,1,0:T(8,128)S(1)}, f32[2,6,768,128]{3,2,1,0:T(8,128)S(1)}, f32[2,768,128]{2,1,0:T(8,128)S(1)}, f32[2,512,128]{2,1,0:T(8,12...) custom-call(s32[1,9]{1,0:T(1,128)S(1)} %add_bitcast_fusion.info, ...), custom_call_target="tpu_custom_call", output_to_operand_aliasing={{0}: (7, {}), {1}: (8, {})} | custom-call | flops 10000000000 | bytes 10000000 | tf_op jit(solution)/shard_map/pallas_call | solution.py:382
  45.7 0.7 collective-permute-start.7
  46.3 1.9 %collective-permute-done.7.in_e = f32[2,768,128]{2,1,0:T(8,128)S(1)} collective-permute-done((f32[2,768,128]{2,1,0:T(8,128)S(1)}, f32[2,768,128]{2,1,0:T(8,128)S(1)}, u32[]{:S(2)}, u32[]{:S(2)}) %collective-permute-start.7) | collective-permute-done | bytes 786464 | tf_op jit(solution)/shard_map/ppermute | solution.py:305
  48.3 0.1 shard_map.80
  48.4 0.1 collective-permute-start.8
  48.4 1.9 %collective-permute-start.9 = (f32[2,4,128,128]{3,2,1,0:T(8,128)S(1)}, f32[2,4,128,128]{3,2,1,0:T(8,128)S(1)}, u32[]{:S(2)}, u32[]{:S(2)}) collective-permute-start(f32[2,4,128,128]{3,2,1,0:T(8,128)S(1)} %get-tuple-element.40), channel_id=1, source_target_pairs={{1,2},{2,1},{5,6},{6,5},{9,10},{10,9},{13,14},{14,13},{17,18},{18,... | collective-permute-start | bytes 1572872 | tf_op jit(solution)/shard_map/ppermute | solution.py:305
  50.4 4.8 %collective-permute-start.6 = (f32[2,512,128]{2,1,0:T(8,128)S(1)}, f32[2,512,128]{2,1,0:T(8,128)S(1)}, u32[]{:S(2)}, u32[]{:S(2)}) collective-permute-start(f32[2,512,128]{2,1,0:T(8,128)S(1)} %get-tuple-element.37), channel_id=1, source_target_pairs={{4,8},{12,16},{20,24},{8,4},{16,12},{24,20},{5,9},{13,17},{21,25},... | collective-permute-start | bytes 1572872 | tf_op jit(solution)/shard_map/ppermute | solution.py:305
  55.2 1.9 %collective-permute-start.10 = (f32[2,128,128]{2,1,0:T(8,128)S(1)}, f32[2,128,128]{2,1,0:T(8,128)S(1)}, u32[]{:S(2)}, u32[]{:S(2)}) collective-permute-start(f32[2,128,128]{2,1,0:T(8,128)S(1)} %get-tuple-element.41), channel_id=1, source_target_pairs={{4,9},{12,17},{20,25},{8,5},{16,13},{24,21},{5,8},{13,16},{21,24},... | collective-permute-start | bytes 393224 | tf_op jit(solution)/shard_map/ppermute | solution.py:305
  57.1 4.2 %collective-permute-start.11 = (f32[2,128,128]{2,1,0:T(8,128)S(1)}, f32[2,128,128]{2,1,0:T(8,128)S(1)}, u32[]{:S(2)}, u32[]{:S(2)}) collective-permute-start(f32[2,128,128]{2,1,0:T(8,128)S(1)} %get-tuple-element.42), channel_id=1, source_target_pairs={{5,10},{13,18},{21,26},{9,6},{17,14},{25,22},{6,9},{14,17},{22,25}... | collective-permute-start | bytes 393224 | tf_op jit(solution)/shard_map/ppermute | solution.py:305
  61.3 0.2 collective-permute-done.8.first
  61.5 1.9 %collective-permute-done.9.second = f32[2,4,128,128]{3,2,1,0:T(8,128)S(1)} collective-permute-done((f32[2,4,128,128]{3,2,1,0:T(8,128)S(1)}, f32[2,4,128,128]{3,2,1,0:T(8,128)S(1)}, u32[]{:S(2)}, u32[]{:S(2)}) %collective-permute-start.9) | collective-permute-done | bytes 524320 | tf_op jit(solution)/shard_map/ppermute | solution.py:305
  63.4 1.4 %shard_map.81.out_in = f32[2,512,512]{2,1,0:T(8,128)} custom-call(f32[2,6,768,128]{3,2,1,0:T(8,128)S(1)} %get-tuple-element.36.acc, f32[2,768,128]{2,1,0:T(8,128)S(1)} %collective-permute-done.7.in_e, f32[2,4,128,128]{3,2,1,0:T(8,128)S(1)} %collective-permute-done.8.first, f32[2,4,128,128]{3,2,1,0:T(8,128)S(1)} %collective-permute-done.9.second), custom_call_target="tpu_custom_call" | custom-call | tf_op jit(solution)/shard_map/pallas_call | solution.py:403
  64.9 0.0 collective-permute-done.10.c_first
  64.9 2.7 %collective-permute-done.11.c_second = f32[2,128,128]{2,1,0:T(8,128)S(1)} collective-permute-done((f32[2,128,128]{2,1,0:T(8,128)S(1)}, f32[2,128,128]{2,1,0:T(8,128)S(1)}, u32[]{:S(2)}, u32[]{:S(2)}) %collective-permute-start.11) | collective-permute-done | bytes 131104 | tf_op jit(solution)/shard_map/ppermute | solution.py:305
  67.5 4.9 %collective-permute-done.6.in_o = f32[2,512,128]{2,1,0:T(8,128)S(1)} collective-permute-done((f32[2,512,128]{2,1,0:T(8,128)S(1)}, f32[2,512,128]{2,1,0:T(8,128)S(1)}, u32[]{:S(2)}, u32[]{:S(2)}) %collective-permute-start.6) | collective-permute-done | bytes 524320 | tf_op jit(solution)/shard_map/ppermute | solution.py:305
  72.4 0.9 %shard_map.82 = f32[2,512,512]{2,1,0:T(8,128)} custom-call(f32[2,6,768,128]{3,2,1,0:T(8,128)S(1)} %get-tuple-element.36.acc, f32[2,512,128]{2,1,0:T(8,128)S(1)} %collective-permute-done.6.in_o, f32[2,4,128,128]{3,2,1,0:T(8,128)S(1)} %collective-permute-done.8.first, ...), custom_call_target="tpu_custom_call", output_to_operand_aliasing={{}: (6, {})} | custom-call | tf_op jit(solution)/shard_map/pallas_call | solution.py:410
Async XLA Ops:
  0.0 23.5 %copy-start = (s32[1,1,4,2]{2,3,1,0:T(2,128)S(1)}, s32[1,1,4,2]{2,3,1,0:T(2,128)}, u32[]{:S(2)}) copy-start(s32[1,1,4,2]{2,3,1,0:T(2,128)} %param.9) | copy-start | bytes 100
  1.2 12.9 %collective-permute-start.1 = (f32[2,128,512]{2,1,0:T(8,128)S(1)}, f32[2,128,512]{2,1,0:T(8,128)S(1)}, u32[]{:S(2)}, u32[]{:S(2)}) collective-permute-start(f32[2,128,512]{2,1,0:T(8,128)S(1)} %get-tuple-element.24), channel_id=1, source_target_pairs={{0,1},{1,0},{2,3},{3,2},{4,5},{5,4},{6,7},{7,6},{8,9},{9,8},{10,11... | collective-permute-start | bytes 1572872 | tf_op jit(solution)/shard_map/ppermute | solution.py:305
  1.5 15.7 %collective-permute-start.2 = (f32[2,128,512]{2,1,0:T(8,128)S(1)}, f32[2,128,512]{2,1,0:T(8,128)S(1)}, u32[]{:S(2)}, u32[]{:S(2)}) collective-permute-start(f32[2,128,512]{2,1,0:T(8,128)S(1)} %get-tuple-element.25), channel_id=1, source_target_pairs={{1,2},{2,1},{5,6},{6,5},{9,10},{10,9},{13,14},{14,13},{17,18},{18,... | collective-permute-start | bytes 1572872 | tf_op jit(solution)/shard_map/ppermute | solution.py:305
  6.9 25.3 %collective-permute-start.4 = (f32[2,512,128]{2,1,0:T(8,128)S(1)}, f32[2,512,128]{2,1,0:T(8,128)S(1)}, u32[]{:S(2)}, u32[]{:S(2)}) collective-permute-start(f32[2,512,128]{2,1,0:T(8,128)S(1)} %shard_map.77), channel_id=1, source_target_pairs={{0,4},{4,0},{8,12},{12,8},{16,20},{20,16},{24,28},{28,24},{1,5},{5... | collective-permute-start | bytes 1572872 | tf_op jit(solution)/shard_map/ppermute | solution.py:305
  17.9 14.3 %collective-permute-start.5 = (f32[2,2,128,128]{3,2,1,0:T(8,128)}, f32[2,2,128,128]{3,2,1,0:T(8,128)}, u32[]{:S(2)}, u32[]{:S(2)}) collective-permute-start(f32[2,2,128,128]{3,2,1,0:T(8,128)} %get-tuple-element.31), channel_id=1, source_target_pairs={{0,4},{4,0},{8,12},{12,8},{16,20},{20,16},{24,28},{28,24},{1,5},{5... | collective-permute-start | bytes 786440 | tf_op jit(solution)/shard_map/ppermute | solution.py:305
  20.5 20.0 %collective-permute-start = (f32[2,512,128]{2,1,0:T(8,128)S(1)}, f32[2,512,128]{2,1,0:T(8,128)S(1)}, u32[]{:S(2)}, u32[]{:S(2)}) collective-permute-start(f32[2,512,128]{2,1,0:T(8,128)S(1)} %shard_map.73), channel_id=1, source_target_pairs={{4,8},{12,16},{20,24},{8,4},{16,12},{24,20},{5,9},{13,17},{21,25},... | collective-permute-start | bytes 1572872 | tf_op jit(solution)/shard_map/ppermute | solution.py:305
  28.7 13.8 %collective-permute-start.3 = (f32[2,2,128,128]{3,2,1,0:T(8,128)S(1)}, f32[2,2,128,128]{3,2,1,0:T(8,128)S(1)}, u32[]{:S(2)}, u32[]{:S(2)}) collective-permute-start(f32[2,2,128,128]{3,2,1,0:T(8,128)S(1)} %get-tuple-element.26), channel_id=1, source_target_pairs={{4,8},{12,16},{20,24},{8,4},{16,12},{24,20},{5,9},{13,17},{21,25},... | collective-permute-start | bytes 786440 | tf_op jit(solution)/shard_map/ppermute | solution.py:305
  45.7 2.6 %collective-permute-start.7 = (f32[2,768,128]{2,1,0:T(8,128)S(1)}, f32[2,768,128]{2,1,0:T(8,128)S(1)}, u32[]{:S(2)}, u32[]{:S(2)}) collective-permute-start(f32[2,768,128]{2,1,0:T(8,128)S(1)} %get-tuple-element.38), channel_id=1, source_target_pairs={{0,4},{4,0},{8,12},{12,8},{16,20},{20,16},{24,28},{28,24},{1,5},{5... | collective-permute-start | bytes 2359304 | tf_op jit(solution)/shard_map/ppermute | solution.py:305
  48.4 13.2 %collective-permute-start.8 = (f32[2,4,128,128]{3,2,1,0:T(8,128)S(1)}, f32[2,4,128,128]{3,2,1,0:T(8,128)S(1)}, u32[]{:S(2)}, u32[]{:S(2)}) collective-permute-start(f32[2,4,128,128]{3,2,1,0:T(8,128)S(1)} %get-tuple-element.39), channel_id=1, source_target_pairs={{0,1},{1,0},{2,3},{3,2},{4,5},{5,4},{6,7},{7,6},{8,9},{9,8},{10,11... | collective-permute-start | bytes 1572872 | tf_op jit(solution)/shard_map/ppermute | solution.py:305
  48.4 15.0 %collective-permute-start.9 = (f32[2,4,128,128]{3,2,1,0:T(8,128)S(1)}, f32[2,4,128,128]{3,2,1,0:T(8,128)S(1)}, u32[]{:S(2)}, u32[]{:S(2)}) collective-permute-start(f32[2,4,128,128]{3,2,1,0:T(8,128)S(1)} %get-tuple-element.40), channel_id=1, source_target_pairs={{1,2},{2,1},{5,6},{6,5},{9,10},{10,9},{13,14},{14,13},{17,18},{18,... | collective-permute-start | bytes 1572872 | tf_op jit(solution)/shard_map/ppermute | solution.py:305
  50.4 22.1 %collective-permute-start.6 = (f32[2,512,128]{2,1,0:T(8,128)S(1)}, f32[2,512,128]{2,1,0:T(8,128)S(1)}, u32[]{:S(2)}, u32[]{:S(2)}) collective-permute-start(f32[2,512,128]{2,1,0:T(8,128)S(1)} %get-tuple-element.37), channel_id=1, source_target_pairs={{4,8},{12,16},{20,24},{8,4},{16,12},{24,20},{5,9},{13,17},{21,25},... | collective-permute-start | bytes 1572872 | tf_op jit(solution)/shard_map/ppermute | solution.py:305
  55.2 9.7 %collective-permute-start.10 = (f32[2,128,128]{2,1,0:T(8,128)S(1)}, f32[2,128,128]{2,1,0:T(8,128)S(1)}, u32[]{:S(2)}, u32[]{:S(2)}) collective-permute-start(f32[2,128,128]{2,1,0:T(8,128)S(1)} %get-tuple-element.41), channel_id=1, source_target_pairs={{4,9},{12,17},{20,25},{8,5},{16,13},{24,21},{5,8},{13,16},{21,24},... | collective-permute-start | bytes 393224 | tf_op jit(solution)/shard_map/ppermute | solution.py:305
  57.1 10.4 %collective-permute-start.11 = (f32[2,128,128]{2,1,0:T(8,128)S(1)}, f32[2,128,128]{2,1,0:T(8,128)S(1)}, u32[]{:S(2)}, u32[]{:S(2)}) collective-permute-start(f32[2,128,128]{2,1,0:T(8,128)S(1)} %get-tuple-element.42), channel_id=1, source_target_pairs={{5,10},{13,18},{21,26},{9,6},{17,14},{25,22},{6,9},{14,17},{22,25}... | collective-permute-start | bytes 393224 | tf_op jit(solution)/shard_map/ppermute | solution.py:305

commit v2 on v1

--- a/solution.py
+++ b/solution.py
@@ -88,7 +88,7 @@
         corner_o[i] = strip[:, :, pl.ds(pl.multiple_of(block_o * LANE, LANE), LANE)]
 
 
-def prepare_kernel(info, measured_h, own, probe, big, small, amp, ext, acc, probe_v, big_v, small_v, measured, sem):
+def prepare_kernel(pos, count, measured_h, own, probe, big, small, amp, ext, acc, probe_v, big_v, small_v, measured, sem):
     slots, width, _ = measured.shape
     half = width // 2
     rows = own.shape[1]
@@ -115,13 +115,13 @@
         cp.wait()
 
 
-def one_frame(slot, info, ext, acc, probe, amp, big, small, patch, x, y, xa, xb, u, v, wave, factor):
+def one_frame(slot, pos, ext, acc, probe, amp, big, small, patch, x, y, xa, xb, u, v, wave, factor):
     modes, _, width, _ = probe.shape
     h = width // 2
     chunk = 64
     lo, hi = slice(0, h), slice(h, width)
-    r = info[0, 1 + 2 * slot]
-    c = info[0, 2 + 2 * slot]
+    r = pos[0, slot]
+    c = pos[1, slot]
     q = jnp.minimum(c // LANE, ext.shape[1] - 3)
     s = c - q * LANE
     left = jnp.bitwise_and(LANE - s, LANE - 1)
@@ -190,27 +190,27 @@
             acc[ch, q + 2, rows, :] += jnp.where(first, g1, zero)
 
 
-def frame_stage(slot, info, cols, width):
-    c = info[0, 2 + 2 * slot]
+def frame_stage(slot, pos, cols, width):
+    c = pos[1, slot]
     odd = lax.rem(lax.axis_index("gx"), 2) == 1
     return jnp.where(odd, c > cols + HALO - width, c < HALO).astype(jnp.int32)
 
 
-def run_frames(stage, info, ext, acc, probe, amp, big, small, *scratch):
+def run_frames(stage, pos, count, ext, acc, probe, amp, big, small, *scratch):
     width = probe.shape[-1]
     cols = (ext.shape[1] - 2) * LANE
 
     def step(slot, carry):
-        @pl.when(frame_stage(slot, info, cols, width) == stage)
+        @pl.when(frame_stage(slot, pos, cols, width) == stage)
         def _():
-            one_frame(slot, info, ext, acc, probe, amp, big, small, *scratch)
+            one_frame(slot, pos, ext, acc, probe, amp, big, small, *scratch)
 
         return carry
 
-    lax.fori_loop(0, info[0, 0], step, 0)
-
-
-def near_kernel(info, first, second, in_e, c_e, probe, amp, big, small, ext_in, acc_in, ext, acc, *rest):
+    lax.fori_loop(0, count[0, 0], step, 0)
+
+
+def near_kernel(pos, count, first, second, in_e, c_e, probe, amp, big, small, ext_in, acc_in, ext, acc, *rest):
     blocks = ext.shape[1] - 2
     rows = ext.shape[2] - 2 * HALO
     col_e, _ = sides(blocks)
@@ -221,10 +221,10 @@
             ext[ch, col_e, pl.ds(at, HALO)] = c_e[i, ch]
     for ch in range(2):
         ext[ch, col_e, HALO : HALO + rows] = in_e[ch]
-    run_frames(0, info, ext, acc, probe, amp, big, small, *rest)
-
-
-def outer_kernel(info, in_o, c_o, probe, amp, big, small, ext_in, acc_in,
+    run_frames(0, pos, count, ext, acc, probe, amp, big, small, *rest)
+
+
+def outer_kernel(pos, count, in_o, c_o, probe, amp, big, small, ext_in, acc_in,
                  ext, acc, rim_e, rim_o, rim_first, rim_second, *rest):
     blocks = ext.shape[1] - 2
     rows = ext.shape[2] - 2 * HALO
@@ -234,7 +234,7 @@
         for i, at in enumerate(offsets):
             ext[ch, col_o, pl.ds(at, HALO)] = c_o[i, ch]
         ext[ch, col_o, HALO : HALO + rows] = in_o[ch]
-    run_frames(1, info, ext, acc, probe, amp, big, small, *rest)
+    run_frames(1, pos, count, ext, acc, probe, amp, big, small, *rest)
     for ch in range(2):
         rim_e[ch] = acc[ch, col_e]
         for at, rim in zip(offsets, (rim_first, rim_second)):
@@ -313,7 +313,7 @@
     n_gx = lax.axis_size("gx")
     n_gy = lax.axis_size("gy")
     slots = measured.shape[2]
-    info = jnp.concatenate([frame_count.reshape(1), positions.reshape(2 * slots)]).reshape(1, -1)
+    pos = jnp.swapaxes(positions, 2, 3).reshape(2, slots)
     object_field, probe, measured = [pltpu.with_memory_space_constraint(a, pltpu.HBM) for a in (object_field, probe, measured[0, 0])]
     pairs_e = [(i, i ^ 1) for i in range(n_gx) if i ^ 1 < n_gx]
     pairs_o = [(i, i + 1) for i in range(1, n_gx - 1, 2)]
@@ -341,7 +341,7 @@
     ext_shape = (2, blocks + 2, rows + 2 * HALO, LANE)
     amp, ext, acc, probe, big, small = call(
         prepare_kernel,
-        [SM] + [HB] * 5,
+        [SM] * 2 + [HB] * 5,
         [VM] * 6,
         [shape(measured.shape), shape(ext_shape), shape(ext_shape), shape(probe.shape),
          jax.ShapeDtypeStruct(big.shape, BF16), jax.ShapeDtypeStruct(small.shape, BF16)],
@@ -349,7 +349,7 @@
         limit=24 << 20,
         flops=10**9,
         moved=10**7,
-    )(info, measured, object_field, probe, big, small)
+    )(pos, frame_count, measured, object_field, probe, big, small)
 
     corner = shape((2, 2, HALO, HALO))
     corner_e, corner_o = call(corners_kernel, [VM] * 2, [VM] * 2, [corner] * 2)(first, second)
@@ -369,27 +369,27 @@
     ]
     ext, acc = call(
         near_kernel,
-        [SM] + [VM] * 10,
+        [SM] * 2 + [VM] * 10,
         [VM] * 2,
         [shape(ext_shape)] * 2,
         work,
         limit=32 << 20,
         flops=10**10,
         moved=10**7,
-        aliases={9: 0, 10: 1},
-    )(info, first, second, in_e, c_e, probe, amp, big, small, ext, acc)
+        aliases={10: 0, 11: 1},
+    )(pos, frame_count, first, second, in_e, c_e, probe, amp, big, small, ext, acc)
     piece = shape((2, HALO, HALO))
     _, acc, rim_e, rim_o, rim_1, rim_2 = call(
         outer_kernel,
-        [SM] + [VM] * 8,
+        [SM] * 2 + [VM] * 8,
         [VM] * 6,
         [shape(ext_shape)] * 2 + [shape((2, rows + 2 * HALO, HALO)), edge, piece, piece],
         work,
         limit=32 << 20,
         flops=10**10,
         moved=10**7,
-        aliases={7: 0, 8: 1},
-    )(info, in_o, c_o, probe, amp, big, small, ext, acc)
+        aliases={8: 0, 9: 1},
+    )(pos, frame_count, in_o, c_o, probe, amp, big, small, ext, acc)
 
     back_e = shift(rim_e, "gx", pairs_e)
     back_o = shift(rim_o, "gx", pairs_o)

time: 74 us -> 73.3 us (level)
  Pallas kernels: 22.3 us -> 21.2 us
  transfers between devices with their start and end apart: 12 -> 12, of which waited for: 8 -> 8; matrix products, arithmetic and copies ran while one was open for 0% -> 0% of each run, Pallas kernels for 23% -> 22%
where the time goes in v2:
time: 73.3 us; the launch traced here: 72.7 us
  starting transfers between devices  27.5 us (38%)
  waiting for transfers between devices  23.2 us (32%)
  Pallas kernels  21.2 us (29%)
  between operations  0.82 us (1%)
    ppermute x12, starting transfers between devices, shift(): return lax.ppermute(array, axis, pairs)  27.5 us
    ppermute x12, waiting for transfers between devices, shift(): return lax.ppermute(array, axis, pairs)  23.2 us
    pallas_call x1, Pallas kernels, program(): call(near_kernel, [SM] * 2 + [VM] * 10, [VM] * 2, [shape(ext_shape)] * 2,...  7.95 us
    pallas_call x1, Pallas kernels, program(): call(prepare_kernel, [SM] * 2 + [HB] * 5, [VM] * 6, [shape(measured.shape...  4.27 us
    pallas_call x1, Pallas kernels, program(): call(outer_kernel, [SM] * 2 + [VM] * 8, [VM] * 6, [shape(ext_shape)] * 2...  3.18 us
  transfers between devices with their start and end apart: 12, of which 8 were waited for; matrix products, arithmetic and copies ran while one was open for 0% of the time, Pallas kernels for 22%

profile of v2, /device:TPU:11, one launch (start us, length us, event | category | flops | bytes accessed | tf_op | source)
XLA Modules:
  0.0 72.7 jit_solution(1153341849581177004)
XLA Ops:
  0.0 0.0 copy-start
  0.0 1.2 %shard_map.74 = (f32[2,128,512]{2,1,0:T(8,128)S(1)}, f32[2,128,512]{2,1,0:T(8,128)S(1)}) custom-call(f32[2,512,512]{2,1,0:T(8,128)} %refs_0_.3), custom_call_target="tpu_custom_call" | custom-call | tf_op jit(solution)/shard_map/pallas_call | solution.py:335
  1.2 0.2 collective-permute-start.1
  1.5 4.3 %collective-permute-start.2 = (f32[2,128,512]{2,1,0:T(8,128)S(1)}, f32[2,128,512]{2,1,0:T(8,128)S(1)}, u32[]{:S(2)}, u32[]{:S(2)}) collective-permute-start(f32[2,128,512]{2,1,0:T(8,128)S(1)} %get-tuple-element.25), channel_id=1, source_target_pairs={{1,2},{2,1},{5,6},{6,5},{9,10},{10,9},{13,14},{14,13},{17,18},{18,... | collective-permute-start | bytes 1572872 | tf_op jit(solution)/shard_map/ppermute | solution.py:305
  5.8 1.1 %shard_map.77 = f32[2,512,128]{2,1,0:T(8,128)S(1)} custom-call(f32[2,512,512]{2,1,0:T(8,128)} %refs_0_.3), custom_call_target="tpu_custom_call" | custom-call | tf_op jit(solution)/shard_map/pallas_call | solution.py:339
  6.9 1.3 %collective-permute-start.4 = (f32[2,512,128]{2,1,0:T(8,128)S(1)}, f32[2,512,128]{2,1,0:T(8,128)S(1)}, u32[]{:S(2)}, u32[]{:S(2)}) collective-permute-start(f32[2,512,128]{2,1,0:T(8,128)S(1)} %shard_map.77), channel_id=1, source_target_pairs={{0,4},{4,0},{8,12},{12,8},{16,20},{20,16},{24,28},{28,24},{1,5},{5... | collective-permute-start | bytes 1572872 | tf_op jit(solution)/shard_map/ppermute | solution.py:305
  8.2 5.9 %collective-permute-done.1.first = f32[2,128,512]{2,1,0:T(8,128)S(1)} collective-permute-done((f32[2,128,512]{2,1,0:T(8,128)S(1)}, f32[2,128,512]{2,1,0:T(8,128)S(1)}, u32[]{:S(2)}, u32[]{:S(2)}) %collective-permute-start.1) | collective-permute-done | bytes 524320 | tf_op jit(solution)/shard_map/ppermute | solution.py:305
  14.1 3.0 %collective-permute-done.2.second = f32[2,128,512]{2,1,0:T(8,128)S(1)} collective-permute-done((f32[2,128,512]{2,1,0:T(8,128)S(1)}, f32[2,128,512]{2,1,0:T(8,128)S(1)}, u32[]{:S(2)}, u32[]{:S(2)}) %collective-permute-start.2) | collective-permute-done | bytes 524320 | tf_op jit(solution)/shard_map/ppermute | solution.py:305
  17.1 0.1 shard_map.75
  17.2 1.6 %collective-permute-start.5 = (f32[2,2,128,128]{3,2,1,0:T(8,128)S(1)}, f32[2,2,128,128]{3,2,1,0:T(8,128)S(1)}, u32[]{:S(2)}, u32[]{:S(2)}) collective-permute-start(f32[2,2,128,128]{3,2,1,0:T(8,128)S(1)} %get-tuple-element.31), channel_id=1, source_target_pairs={{0,4},{4,0},{8,12},{12,8},{16,20},{20,16},{24,28},{28,24},{1,5},{5... | collective-permute-start | bytes 786440 | tf_op jit(solution)/shard_map/ppermute | solution.py:305
  18.8 1.0 %shard_map.73 = f32[2,512,128]{2,1,0:T(8,128)S(1)} custom-call(f32[2,512,512]{2,1,0:T(8,128)} %refs_0_.3), custom_call_target="tpu_custom_call" | custom-call | tf_op jit(solution)/shard_map/pallas_call | solution.py:338
  19.9 3.0 %collective-permute-start = (f32[2,512,128]{2,1,0:T(8,128)S(1)}, f32[2,512,128]{2,1,0:T(8,128)S(1)}, u32[]{:S(2)}, u32[]{:S(2)}) collective-permute-start(f32[2,512,128]{2,1,0:T(8,128)S(1)} %shard_map.73), channel_id=1, source_target_pairs={{4,8},{12,16},{20,24},{8,4},{16,12},{24,20},{5,9},{13,17},{21,25},... | collective-permute-start | bytes 1572872 | tf_op jit(solution)/shard_map/ppermute | solution.py:305
  23.5 0.0 copy-done
  23.6 4.3 %shard_map.76 = (f32[4,256,256]{2,1,0:T(8,128)S(1)}, f32[2,6,768,128]{3,2,1,0:T(8,128)S(1)}, f32[2,6,768,128]{3,2,1,0:T(8,128)S(1)}, f32[3,2,256,256]{3,2,1,0:T(...) custom-call(s32[2,4]{1,0:T(2,128)S(1)} %bitcast.4, s32[1,1]{1,0:T(1,128)S(6)} %copy.18.count, ...), custom_call_target="tpu_custom_call" | custom-call | flops 1000000000 | bytes 10000000 | tf_op jit(solution)/shard_map/pallas_call | solution.py:342
  27.8 3.4 %collective-permute-start.3 = (f32[2,2,128,128]{3,2,1,0:T(8,128)S(1)}, f32[2,2,128,128]{3,2,1,0:T(8,128)S(1)}, u32[]{:S(2)}, u32[]{:S(2)}) collective-permute-start(f32[2,2,128,128]{3,2,1,0:T(8,128)S(1)} %get-tuple-element.26), channel_id=1, source_target_pairs={{4,8},{12,16},{20,24},{8,4},{16,12},{24,20},{5,9},{13,17},{21,25},... | collective-permute-start | bytes 786440 | tf_op jit(solution)/shard_map/ppermute | solution.py:305
  31.3 0.0 collective-permute-done.4.in_e
  31.3 0.0 collective-permute-done.5.c_e
  31.3 8.0 %shard_map.78 = (f32[2,6,768,128]{3,2,1,0:T(8,128)S(1)}, f32[2,6,768,128]{3,2,1,0:T(8,128)S(1)}) custom-call(s32[2,4]{1,0:T(2,128)S(1)} %bitcast.5, s32[1,1]{1,0:T(1,128)S(6)} %copy.18.count, f32[2,128,512]{2,1,0:T(8,128)S(1)} %collective-permute-done.1.first, ...), custom_call_target="tpu_custom_call", output_to_operand_aliasing={{0}: (10, {}), {1}: (11, {})} | custom-call | flops 10000000000 | bytes 10000000 | tf_op jit(solution)/shard_map/pallas_call | solution.py:370
  39.3 0.0 collective-permute-done.in_o
  39.3 2.6 %collective-permute-done.3.c_o = f32[2,2,128,128]{3,2,1,0:T(8,128)S(1)} collective-permute-done((f32[2,2,128,128]{3,2,1,0:T(8,128)S(1)}, f32[2,2,128,128]{3,2,1,0:T(8,128)S(1)}, u32[]{:S(2)}, u32[]{:S(2)}) %collective-permute-start.3) | collective-permute-done | bytes 262176 | tf_op jit(solution)/shard_map/ppermute | solution.py:305
  41.9 3.2 %shard_map.79 = (f32[2,6,768,128]{3,2,1,0:T(8,128)S(1)}, f32[2,6,768,128]{3,2,1,0:T(8,128)S(1)}, f32[2,768,128]{2,1,0:T(8,128)S(1)}, f32[2,512,128]{2,1,0:T(8,12...) custom-call(s32[2,4]{1,0:T(2,128)S(1)} %bitcast.6, ...), custom_call_target="tpu_custom_call", output_to_operand_aliasing={{0}: (8, {}), {1}: (9, {})} | custom-call | flops 10000000000 | bytes 10000000 | tf_op jit(solution)/shard_map/pallas_call | solution.py:382
  45.1 0.6 collective-permute-start.7
  45.7 1.9 %collective-permute-done.7.in_e = f32[2,768,128]{2,1,0:T(8,128)S(1)} collective-permute-done((f32[2,768,128]{2,1,0:T(8,128)S(1)}, f32[2,768,128]{2,1,0:T(8,128)S(1)}, u32[]{:S(2)}, u32[]{:S(2)}) %collective-permute-start.7) | collective-permute-done | bytes 786464 | tf_op jit(solution)/shard_map/ppermute | solution.py:305
  47.6 0.1 shard_map.80
  47.7 0.1 collective-permute-start.8
  47.8 1.9 %collective-permute-start.9 = (f32[2,4,128,128]{3,2,1,0:T(8,128)S(1)}, f32[2,4,128,128]{3,2,1,0:T(8,128)S(1)}, u32[]{:S(2)}, u32[]{:S(2)}) collective-permute-start(f32[2,4,128,128]{3,2,1,0:T(8,128)S(1)} %get-tuple-element.40), channel_id=1, source_target_pairs={{1,2},{2,1},{5,6},{6,5},{9,10},{10,9},{13,14},{14,13},{17,18},{18,... | collective-permute-start | bytes 1572872 | tf_op jit(solution)/shard_map/ppermute | solution.py:305
  49.7 4.8 %collective-permute-start.6 = (f32[2,512,128]{2,1,0:T(8,128)S(1)}, f32[2,512,128]{2,1,0:T(8,128)S(1)}, u32[]{:S(2)}, u32[]{:S(2)}) collective-permute-start(f32[2,512,128]{2,1,0:T(8,128)S(1)} %get-tuple-element.37), channel_id=1, source_target_pairs={{4,8},{12,16},{20,24},{8,4},{16,12},{24,20},{5,9},{13,17},{21,25},... | collective-permute-start | bytes 1572872 | tf_op jit(solution)/shard_map/ppermute | solution.py:305
  54.6 1.9 %collective-permute-start.10 = (f32[2,128,128]{2,1,0:T(8,128)S(1)}, f32[2,128,128]{2,1,0:T(8,128)S(1)}, u32[]{:S(2)}, u32[]{:S(2)}) collective-permute-start(f32[2,128,128]{2,1,0:T(8,128)S(1)} %get-tuple-element.41), channel_id=1, source_target_pairs={{4,9},{12,17},{20,25},{8,5},{16,13},{24,21},{5,8},{13,16},{21,24},... | collective-permute-start | bytes 393224 | tf_op jit(solution)/shard_map/ppermute | solution.py:305
  56.5 4.2 %collective-permute-start.11 = (f32[2,128,128]{2,1,0:T(8,128)S(1)}, f32[2,128,128]{2,1,0:T(8,128)S(1)}, u32[]{:S(2)}, u32[]{:S(2)}) collective-permute-start(f32[2,128,128]{2,1,0:T(8,128)S(1)} %get-tuple-element.42), channel_id=1, source_target_pairs={{5,10},{13,18},{21,26},{9,6},{17,14},{25,22},{6,9},{14,17},{22,25}... | collective-permute-start | bytes 393224 | tf_op jit(solution)/shard_map/ppermute | solution.py:305
  60.7 0.2 collective-permute-done.8.first
  60.9 1.9 %collective-permute-done.9.second = f32[2,4,128,128]{3,2,1,0:T(8,128)S(1)} collective-permute-done((f32[2,4,128,128]{3,2,1,0:T(8,128)S(1)}, f32[2,4,128,128]{3,2,1,0:T(8,128)S(1)}, u32[]{:S(2)}, u32[]{:S(2)}) %collective-permute-start.9) | collective-permute-done | bytes 524320 | tf_op jit(solution)/shard_map/ppermute | solution.py:305
  62.8 1.4 %shard_map.81.out_in = f32[2,512,512]{2,1,0:T(8,128)} custom-call(f32[2,6,768,128]{3,2,1,0:T(8,128)S(1)} %get-tuple-element.36.acc, f32[2,768,128]{2,1,0:T(8,128)S(1)} %collective-permute-done.7.in_e, f32[2,4,128,128]{3,2,1,0:T(8,128)S(1)} %collective-permute-done.8.first, f32[2,4,128,128]{3,2,1,0:T(8,128)S(1)} %collective-permute-done.9.second), custom_call_target="tpu_custom_call" | custom-call | tf_op jit(solution)/shard_map/pallas_call | solution.py:403
  64.2 0.0 collective-permute-done.10.c_first
  64.2 2.7 %collective-permute-done.11.c_second = f32[2,128,128]{2,1,0:T(8,128)S(1)} collective-permute-done((f32[2,128,128]{2,1,0:T(8,128)S(1)}, f32[2,128,128]{2,1,0:T(8,128)S(1)}, u32[]{:S(2)}, u32[]{:S(2)}) %collective-permute-start.11) | collective-permute-done | bytes 131104 | tf_op jit(solution)/shard_map/ppermute | solution.py:305
  66.9 4.9 %collective-permute-done.6.in_o = f32[2,512,128]{2,1,0:T(8,128)S(1)} collective-permute-done((f32[2,512,128]{2,1,0:T(8,128)S(1)}, f32[2,512,128]{2,1,0:T(8,128)S(1)}, u32[]{:S(2)}, u32[]{:S(2)}) %collective-permute-start.6) | collective-permute-done | bytes 524320 | tf_op jit(solution)/shard_map/ppermute | solution.py:305
  71.8 0.9 %shard_map.82 = f32[2,512,512]{2,1,0:T(8,128)} custom-call(f32[2,6,768,128]{3,2,1,0:T(8,128)S(1)} %get-tuple-element.36.acc, f32[2,512,128]{2,1,0:T(8,128)S(1)} %collective-permute-done.6.in_o, f32[2,4,128,128]{3,2,1,0:T(8,128)S(1)} %collective-permute-done.8.first, ...), custom_call_target="tpu_custom_call", output_to_operand_aliasing={{}: (6, {})} | custom-call | tf_op jit(solution)/shard_map/pallas_call | solution.py:410
Async XLA Ops:
  0.0 23.6 %copy-start = (s32[1,1,4,2]{2,3,1,0:T(2,128)S(1)}, s32[1,1,4,2]{2,3,1,0:T(2,128)}, u32[]{:S(2)}) copy-start(s32[1,1,4,2]{2,3,1,0:T(2,128)} %param.9) | copy-start | bytes 100
  1.2 12.9 %collective-permute-start.1 = (f32[2,128,512]{2,1,0:T(8,128)S(1)}, f32[2,128,512]{2,1,0:T(8,128)S(1)}, u32[]{:S(2)}, u32[]{:S(2)}) collective-permute-start(f32[2,128,512]{2,1,0:T(8,128)S(1)} %get-tuple-element.24), channel_id=1, source_target_pairs={{0,1},{1,0},{2,3},{3,2},{4,5},{5,4},{6,7},{7,6},{8,9},{9,8},{10,11... | collective-permute-start | bytes 1572872 | tf_op jit(solution)/shard_map/ppermute | solution.py:305
  1.5 15.7 %collective-permute-start.2 = (f32[2,128,512]{2,1,0:T(8,128)S(1)}, f32[2,128,512]{2,1,0:T(8,128)S(1)}, u32[]{:S(2)}, u32[]{:S(2)}) collective-permute-start(f32[2,128,512]{2,1,0:T(8,128)S(1)} %get-tuple-element.25), channel_id=1, source_target_pairs={{1,2},{2,1},{5,6},{6,5},{9,10},{10,9},{13,14},{14,13},{17,18},{18,... | collective-permute-start | bytes 1572872 | tf_op jit(solution)/shard_map/ppermute | solution.py:305
  6.9 24.4 %collective-permute-start.4 = (f32[2,512,128]{2,1,0:T(8,128)S(1)}, f32[2,512,128]{2,1,0:T(8,128)S(1)}, u32[]{:S(2)}, u32[]{:S(2)}) collective-permute-start(f32[2,512,128]{2,1,0:T(8,128)S(1)} %shard_map.77), channel_id=1, source_target_pairs={{0,4},{4,0},{8,12},{12,8},{16,20},{20,16},{24,28},{28,24},{1,5},{5... | collective-permute-start | bytes 1572872 | tf_op jit(solution)/shard_map/ppermute | solution.py:305
  17.2 14.1 %collective-permute-start.5 = (f32[2,2,128,128]{3,2,1,0:T(8,128)S(1)}, f32[2,2,128,128]{3,2,1,0:T(8,128)S(1)}, u32[]{:S(2)}, u32[]{:S(2)}) collective-permute-start(f32[2,2,128,128]{3,2,1,0:T(8,128)S(1)} %get-tuple-element.31), channel_id=1, source_target_pairs={{0,4},{4,0},{8,12},{12,8},{16,20},{20,16},{24,28},{28,24},{1,5},{5... | collective-permute-start | bytes 786440 | tf_op jit(solution)/shard_map/ppermute | solution.py:305
  19.9 19.4 %collective-permute-start = (f32[2,512,128]{2,1,0:T(8,128)S(1)}, f32[2,512,128]{2,1,0:T(8,128)S(1)}, u32[]{:S(2)}, u32[]{:S(2)}) collective-permute-start(f32[2,512,128]{2,1,0:T(8,128)S(1)} %shard_map.73), channel_id=1, source_target_pairs={{4,8},{12,16},{20,24},{8,4},{16,12},{24,20},{5,9},{13,17},{21,25},... | collective-permute-start | bytes 1572872 | tf_op jit(solution)/shard_map/ppermute | solution.py:305
  27.8 14.1 %collective-permute-start.3 = (f32[2,2,128,128]{3,2,1,0:T(8,128)S(1)}, f32[2,2,128,128]{3,2,1,0:T(8,128)S(1)}, u32[]{:S(2)}, u32[]{:S(2)}) collective-permute-start(f32[2,2,128,128]{3,2,1,0:T(8,128)S(1)} %get-tuple-element.26), channel_id=1, source_target_pairs={{4,8},{12,16},{20,24},{8,4},{16,12},{24,20},{5,9},{13,17},{21,25},... | collective-permute-start | bytes 786440 | tf_op jit(solution)/shard_map/ppermute | solution.py:305
  45.1 2.5 %collective-permute-start.7 = (f32[2,768,128]{2,1,0:T(8,128)S(1)}, f32[2,768,128]{2,1,0:T(8,128)S(1)}, u32[]{:S(2)}, u32[]{:S(2)}) collective-permute-start(f32[2,768,128]{2,1,0:T(8,128)S(1)} %get-tuple-element.38), channel_id=1, source_target_pairs={{0,4},{4,0},{8,12},{12,8},{16,20},{20,16},{24,28},{28,24},{1,5},{5... | collective-permute-start | bytes 2359304 | tf_op jit(solution)/shard_map/ppermute | solution.py:305
  47.7 13.2 %collective-permute-start.8 = (f32[2,4,128,128]{3,2,1,0:T(8,128)S(1)}, f32[2,4,128,128]{3,2,1,0:T(8,128)S(1)}, u32[]{:S(2)}, u32[]{:S(2)}) collective-permute-start(f32[2,4,128,128]{3,2,1,0:T(8,128)S(1)} %get-tuple-element.39), channel_id=1, source_target_pairs={{0,1},{1,0},{2,3},{3,2},{4,5},{5,4},{6,7},{7,6},{8,9},{9,8},{10,11... | collective-permute-start | bytes 1572872 | tf_op jit(solution)/shard_map/ppermute | solution.py:305
  47.8 15.0 %collective-permute-start.9 = (f32[2,4,128,128]{3,2,1,0:T(8,128)S(1)}, f32[2,4,128,128]{3,2,1,0:T(8,128)S(1)}, u32[]{:S(2)}, u32[]{:S(2)}) collective-permute-start(f32[2,4,128,128]{3,2,1,0:T(8,128)S(1)} %get-tuple-element.40), channel_id=1, source_target_pairs={{1,2},{2,1},{5,6},{6,5},{9,10},{10,9},{13,14},{14,13},{17,18},{18,... | collective-permute-start | bytes 1572872 | tf_op jit(solution)/shard_map/ppermute | solution.py:305
  49.7 22.1 %collective-permute-start.6 = (f32[2,512,128]{2,1,0:T(8,128)S(1)}, f32[2,512,128]{2,1,0:T(8,128)S(1)}, u32[]{:S(2)}, u32[]{:S(2)}) collective-permute-start(f32[2,512,128]{2,1,0:T(8,128)S(1)} %get-tuple-element.37), channel_id=1, source_target_pairs={{4,8},{12,16},{20,24},{8,4},{16,12},{24,20},{5,9},{13,17},{21,25},... | collective-permute-start | bytes 1572872 | tf_op jit(solution)/shard_map/ppermute | solution.py:305
  54.6 9.7 %collective-permute-start.10 = (f32[2,128,128]{2,1,0:T(8,128)S(1)}, f32[2,128,128]{2,1,0:T(8,128)S(1)}, u32[]{:S(2)}, u32[]{:S(2)}) collective-permute-start(f32[2,128,128]{2,1,0:T(8,128)S(1)} %get-tuple-element.41), channel_id=1, source_target_pairs={{4,9},{12,17},{20,25},{8,5},{16,13},{24,21},{5,8},{13,16},{21,24},... | collective-permute-start | bytes 393224 | tf_op jit(solution)/shard_map/ppermute | solution.py:305
  56.5 10.4 %collective-permute-start.11 = (f32[2,128,128]{2,1,0:T(8,128)S(1)}, f32[2,128,128]{2,1,0:T(8,128)S(1)}, u32[]{:S(2)}, u32[]{:S(2)}) collective-permute-start(f32[2,128,128]{2,1,0:T(8,128)S(1)} %get-tuple-element.42), channel_id=1, source_target_pairs={{5,10},{13,18},{21,26},{9,6},{17,14},{25,22},{6,9},{14,17},{22,25}... | collective-permute-start | bytes 393224 | tf_op jit(solution)/shard_map/ppermute | solution.py:305

commit v3 on v2

--- a/solution.py
+++ b/solution.py
@@ -143,9 +143,10 @@
                 x[m, rows, cc] = (pr * o_re - pi * o_im).astype(BF16)
                 x[m, rows, slice(width + cc.start, width + cc.stop)] = (pr * o_im + pi * o_re).astype(BF16)
         for k in range(2):
-            e = dot(x[m], big[0, :, k * width : (k + 1) * width])
-            y[m, 0:width, k * h : (k + 1) * h] = e[:, lo].astype(BF16)
-            y[m, width:, k * h : (k + 1) * h] = e[:, hi].astype(BF16)
+            for i in range(0, width, h):
+                e = dot(x[m, i : i + h], big[0, :, k * width : (k + 1) * width])
+                y[m, i : i + h, k * h : (k + 1) * h] = e[:, lo].astype(BF16)
+                y[m, width + i : width + i + h, k * h : (k + 1) * h] = e[:, hi].astype(BF16)
     for m in range(modes):
         for k in range(2):
             p = dot(big[1, k * width : (k + 1) * width], y[m])

time: 73.3 us -> 73.3 us (level)
  no operation moved by 1% of the time
where the time goes in v3:
time: 73.3 us; the launch traced here: 72.7 us
  starting transfers between devices  27.5 us (38%)
  waiting for transfers between devices  23.3 us (32%)
  Pallas kernels  21 us (29%)
  between operations  0.82 us (1%)
    ppermute x12, starting transfers between devices, shift(): return lax.ppermute(array, axis, pairs)  27.5 us
    ppermute x12, waiting for transfers between devices, shift(): return lax.ppermute(array, axis, pairs)  23.3 us
    pallas_call x1, Pallas kernels, program(): call(near_kernel, [SM] * 2 + [VM] * 10, [VM] * 2, [shape(ext_shape)] * 2,...  7.79 us
    pallas_call x1, Pallas kernels, program(): call(prepare_kernel, [SM] * 2 + [HB] * 5, [VM] * 6, [shape(measured.shape...  4.27 us
    pallas_call x1, Pallas kernels, program(): call(outer_kernel, [SM] * 2 + [VM] * 8, [VM] * 6, [shape(ext_shape)] * 2...  3.13 us
  transfers between devices with their start and end apart: 12, of which 8 were waited for; matrix products, arithmetic and copies ran while one was open for 0% of the time, Pallas kernels for 22%

profile of v3, /device:TPU:11, one launch (start us, length us, event | category | flops | bytes accessed | tf_op | source)
XLA Modules:
  0.0 72.7 jit_solution(7983789637959607620)
XLA Ops:
  0.0 0.0 copy-start
  0.0 1.2 %shard_map.74 = (f32[2,128,512]{2,1,0:T(8,128)S(1)}, f32[2,128,512]{2,1,0:T(8,128)S(1)}) custom-call(f32[2,512,512]{2,1,0:T(8,128)} %refs_0_.3), custom_call_target="tpu_custom_call" | custom-call | tf_op jit(solution)/shard_map/pallas_call | solution.py:336
  1.2 0.2 collective-permute-start.1
  1.5 4.3 %collective-permute-start.2 = (f32[2,128,512]{2,1,0:T(8,128)S(1)}, f32[2,128,512]{2,1,0:T(8,128)S(1)}, u32[]{:S(2)}, u32[]{:S(2)}) collective-permute-start(f32[2,128,512]{2,1,0:T(8,128)S(1)} %get-tuple-element.25), channel_id=1, source_target_pairs={{1,2},{2,1},{5,6},{6,5},{9,10},{10,9},{13,14},{14,13},{17,18},{18,... | collective-permute-start | bytes 1572872 | tf_op jit(solution)/shard_map/ppermute | solution.py:306
  5.8 1.1 %shard_map.77 = f32[2,512,128]{2,1,0:T(8,128)S(1)} custom-call(f32[2,512,512]{2,1,0:T(8,128)} %refs_0_.3), custom_call_target="tpu_custom_call" | custom-call | tf_op jit(solution)/shard_map/pallas_call | solution.py:340
  6.9 1.3 %collective-permute-start.4 = (f32[2,512,128]{2,1,0:T(8,128)S(1)}, f32[2,512,128]{2,1,0:T(8,128)S(1)}, u32[]{:S(2)}, u32[]{:S(2)}) collective-permute-start(f32[2,512,128]{2,1,0:T(8,128)S(1)} %shard_map.77), channel_id=1, source_target_pairs={{0,4},{4,0},{8,12},{12,8},{16,20},{20,16},{24,28},{28,24},{1,5},{5... | collective-permute-start | bytes 1572872 | tf_op jit(solution)/shard_map/ppermute | solution.py:306
  8.2 5.9 %collective-permute-done.1.first = f32[2,128,512]{2,1,0:T(8,128)S(1)} collective-permute-done((f32[2,128,512]{2,1,0:T(8,128)S(1)}, f32[2,128,512]{2,1,0:T(8,128)S(1)}, u32[]{:S(2)}, u32[]{:S(2)}) %collective-permute-start.1) | collective-permute-done | bytes 524320 | tf_op jit(solution)/shard_map/ppermute | solution.py:306
  14.1 3.0 %collective-permute-done.2.second = f32[2,128,512]{2,1,0:T(8,128)S(1)} collective-permute-done((f32[2,128,512]{2,1,0:T(8,128)S(1)}, f32[2,128,512]{2,1,0:T(8,128)S(1)}, u32[]{:S(2)}, u32[]{:S(2)}) %collective-permute-start.2) | collective-permute-done | bytes 524320 | tf_op jit(solution)/shard_map/ppermute | solution.py:306
  17.1 0.1 shard_map.75
  17.2 1.6 %collective-permute-start.5 = (f32[2,2,128,128]{3,2,1,0:T(8,128)S(1)}, f32[2,2,128,128]{3,2,1,0:T(8,128)S(1)}, u32[]{:S(2)}, u32[]{:S(2)}) collective-permute-start(f32[2,2,128,128]{3,2,1,0:T(8,128)S(1)} %get-tuple-element.31), channel_id=1, source_target_pairs={{0,4},{4,0},{8,12},{12,8},{16,20},{20,16},{24,28},{28,24},{1,5},{5... | collective-permute-start | bytes 786440 | tf_op jit(solution)/shard_map/ppermute | solution.py:306
  18.8 1.0 %shard_map.73 = f32[2,512,128]{2,1,0:T(8,128)S(1)} custom-call(f32[2,512,512]{2,1,0:T(8,128)} %refs_0_.3), custom_call_target="tpu_custom_call" | custom-call | tf_op jit(solution)/shard_map/pallas_call | solution.py:339
  19.9 3.0 %collective-permute-start = (f32[2,512,128]{2,1,0:T(8,128)S(1)}, f32[2,512,128]{2,1,0:T(8,128)S(1)}, u32[]{:S(2)}, u32[]{:S(2)}) collective-permute-start(f32[2,512,128]{2,1,0:T(8,128)S(1)} %shard_map.73), channel_id=1, source_target_pairs={{4,8},{12,16},{20,24},{8,4},{16,12},{24,20},{5,9},{13,17},{21,25},... | collective-permute-start | bytes 1572872 | tf_op jit(solution)/shard_map/ppermute | solution.py:306
  23.5 0.0 copy-done
  23.6 4.3 %shard_map.76 = (f32[4,256,256]{2,1,0:T(8,128)S(1)}, f32[2,6,768,128]{3,2,1,0:T(8,128)S(1)}, f32[2,6,768,128]{3,2,1,0:T(8,128)S(1)}, f32[3,2,256,256]{3,2,1,0:T(...) custom-call(s32[2,4]{1,0:T(2,128)S(1)} %bitcast.4, s32[1,1]{1,0:T(1,128)S(6)} %copy.18.count, ...), custom_call_target="tpu_custom_call" | custom-call | flops 1000000000 | bytes 10000000 | tf_op jit(solution)/shard_map/pallas_call | solution.py:343
  27.8 3.4 %collective-permute-start.3 = (f32[2,2,128,128]{3,2,1,0:T(8,128)S(1)}, f32[2,2,128,128]{3,2,1,0:T(8,128)S(1)}, u32[]{:S(2)}, u32[]{:S(2)}) collective-permute-start(f32[2,2,128,128]{3,2,1,0:T(8,128)S(1)} %get-tuple-element.26), channel_id=1, source_target_pairs={{4,8},{12,16},{20,24},{8,4},{16,12},{24,20},{5,9},{13,17},{21,25},... | collective-permute-start | bytes 786440 | tf_op jit(solution)/shard_map/ppermute | solution.py:306
  31.3 0.0 collective-permute-done.4.in_e
  31.3 0.0 collective-permute-done.5.c_e
  31.3 7.8 %shard_map.78 = (f32[2,6,768,128]{3,2,1,0:T(8,128)S(1)}, f32[2,6,768,128]{3,2,1,0:T(8,128)S(1)}) custom-call(s32[2,4]{1,0:T(2,128)S(1)} %bitcast.5, s32[1,1]{1,0:T(1,128)S(6)} %copy.18.count, f32[2,128,512]{2,1,0:T(8,128)S(1)} %collective-permute-done.1.first, ...), custom_call_target="tpu_custom_call", output_to_operand_aliasing={{0}: (10, {}), {1}: (11, {})} | custom-call | flops 10000000000 | bytes 10000000 | tf_op jit(solution)/shard_map/pallas_call | solution.py:371
  39.1 0.0 collective-permute-done.in_o
  39.1 2.8 %collective-permute-done.3.c_o = f32[2,2,128,128]{3,2,1,0:T(8,128)S(1)} collective-permute-done((f32[2,2,128,128]{3,2,1,0:T(8,128)S(1)}, f32[2,2,128,128]{3,2,1,0:T(8,128)S(1)}, u32[]{:S(2)}, u32[]{:S(2)}) %collective-permute-start.3) | collective-permute-done | bytes 262176 | tf_op jit(solution)/shard_map/ppermute | solution.py:306
  41.9 3.1 %shard_map.79 = (f32[2,6,768,128]{3,2,1,0:T(8,128)S(1)}, f32[2,6,768,128]{3,2,1,0:T(8,128)S(1)}, f32[2,768,128]{2,1,0:T(8,128)S(1)}, f32[2,512,128]{2,1,0:T(8,12...) custom-call(s32[2,4]{1,0:T(2,128)S(1)} %bitcast.6, ...), custom_call_target="tpu_custom_call", output_to_operand_aliasing={{0}: (8, {}), {1}: (9, {})} | custom-call | flops 10000000000 | bytes 10000000 | tf_op jit(solution)/shard_map/pallas_call | solution.py:383
  45.0 0.6 collective-permute-start.7
  45.6 1.9 %collective-permute-done.7.in_e = f32[2,768,128]{2,1,0:T(8,128)S(1)} collective-permute-done((f32[2,768,128]{2,1,0:T(8,128)S(1)}, f32[2,768,128]{2,1,0:T(8,128)S(1)}, u32[]{:S(2)}, u32[]{:S(2)}) %collective-permute-start.7) | collective-permute-done | bytes 786464 | tf_op jit(solution)/shard_map/ppermute | solution.py:306
  47.5 0.1 shard_map.80
  47.6 0.1 collective-permute-start.8
  47.7 1.9 %collective-permute-start.9 = (f32[2,4,128,128]{3,2,1,0:T(8,128)S(1)}, f32[2,4,128,128]{3,2,1,0:T(8,128)S(1)}, u32[]{:S(2)}, u32[]{:S(2)}) collective-permute-start(f32[2,4,128,128]{3,2,1,0:T(8,128)S(1)} %get-tuple-element.40), channel_id=1, source_target_pairs={{1,2},{2,1},{5,6},{6,5},{9,10},{10,9},{13,14},{14,13},{17,18},{18,... | collective-permute-start | bytes 1572872 | tf_op jit(solution)/shard_map/ppermute | solution.py:306
  49.6 4.9 %collective-permute-start.6 = (f32[2,512,128]{2,1,0:T(8,128)S(1)}, f32[2,512,128]{2,1,0:T(8,128)S(1)}, u32[]{:S(2)}, u32[]{:S(2)}) collective-permute-start(f32[2,512,128]{2,1,0:T(8,128)S(1)} %get-tuple-element.37), channel_id=1, source_target_pairs={{4,8},{12,16},{20,24},{8,4},{16,12},{24,20},{5,9},{13,17},{21,25},... | collective-permute-start | bytes 1572872 | tf_op jit(solution)/shard_map/ppermute | solution.py:306
  54.5 1.9 %collective-permute-start.10 = (f32[2,128,128]{2,1,0:T(8,128)S(1)}, f32[2,128,128]{2,1,0:T(8,128)S(1)}, u32[]{:S(2)}, u32[]{:S(2)}) collective-permute-start(f32[2,128,128]{2,1,0:T(8,128)S(1)} %get-tuple-element.41), channel_id=1, source_target_pairs={{4,9},{12,17},{20,25},{8,5},{16,13},{24,21},{5,8},{13,16},{21,24},... | collective-permute-start | bytes 393224 | tf_op jit(solution)/shard_map/ppermute | solution.py:306
  56.4 4.2 %collective-permute-start.11 = (f32[2,128,128]{2,1,0:T(8,128)S(1)}, f32[2,128,128]{2,1,0:T(8,128)S(1)}, u32[]{:S(2)}, u32[]{:S(2)}) collective-permute-start(f32[2,128,128]{2,1,0:T(8,128)S(1)} %get-tuple-element.42), channel_id=1, source_target_pairs={{5,10},{13,18},{21,26},{9,6},{17,14},{25,22},{6,9},{14,17},{22,25}... | collective-permute-start | bytes 393224 | tf_op jit(solution)/shard_map/ppermute | solution.py:306
  60.7 0.1 collective-permute-done.8.first
  60.8 1.9 %collective-permute-done.9.second = f32[2,4,128,128]{3,2,1,0:T(8,128)S(1)} collective-permute-done((f32[2,4,128,128]{3,2,1,0:T(8,128)S(1)}, f32[2,4,128,128]{3,2,1,0:T(8,128)S(1)}, u32[]{:S(2)}, u32[]{:S(2)}) %collective-permute-start.9) | collective-permute-done | bytes 524320 | tf_op jit(solution)/shard_map/ppermute | solution.py:306
  62.7 1.4 %shard_map.81.out_in = f32[2,512,512]{2,1,0:T(8,128)} custom-call(f32[2,6,768,128]{3,2,1,0:T(8,128)S(1)} %get-tuple-element.36.acc, f32[2,768,128]{2,1,0:T(8,128)S(1)} %collective-permute-done.7.in_e, f32[2,4,128,128]{3,2,1,0:T(8,128)S(1)} %collective-permute-done.8.first, f32[2,4,128,128]{3,2,1,0:T(8,128)S(1)} %collective-permute-done.9.second), custom_call_target="tpu_custom_call" | custom-call | tf_op jit(solution)/shard_map/pallas_call | solution.py:404
  64.1 0.0 collective-permute-done.10.c_first
  64.1 2.7 %collective-permute-done.11.c_second = f32[2,128,128]{2,1,0:T(8,128)S(1)} collective-permute-done((f32[2,128,128]{2,1,0:T(8,128)S(1)}, f32[2,128,128]{2,1,0:T(8,128)S(1)}, u32[]{:S(2)}, u32[]{:S(2)}) %collective-permute-start.11) | collective-permute-done | bytes 131104 | tf_op jit(solution)/shard_map/ppermute | solution.py:306
  66.9 4.9 %collective-permute-done.6.in_o = f32[2,512,128]{2,1,0:T(8,128)S(1)} collective-permute-done((f32[2,512,128]{2,1,0:T(8,128)S(1)}, f32[2,512,128]{2,1,0:T(8,128)S(1)}, u32[]{:S(2)}, u32[]{:S(2)}) %collective-permute-start.6) | collective-permute-done | bytes 524320 | tf_op jit(solution)/shard_map/ppermute | solution.py:306
  71.8 0.9 %shard_map.82 = f32[2,512,512]{2,1,0:T(8,128)} custom-call(f32[2,6,768,128]{3,2,1,0:T(8,128)S(1)} %get-tuple-element.36.acc, f32[2,512,128]{2,1,0:T(8,128)S(1)} %collective-permute-done.6.in_o, f32[2,4,128,128]{3,2,1,0:T(8,128)S(1)} %collective-permute-done.8.first, ...), custom_call_target="tpu_custom_call", output_to_operand_aliasing={{}: (6, {})} | custom-call | tf_op jit(solution)/shard_map/pallas_call | solution.py:411
Async XLA Ops:
  0.0 23.6 %copy-start = (s32[1,1,4,2]{2,3,1,0:T(2,128)S(1)}, s32[1,1,4,2]{2,3,1,0:T(2,128)}, u32[]{:S(2)}) copy-start(s32[1,1,4,2]{2,3,1,0:T(2,128)} %param.9) | copy-start | bytes 100
  1.2 12.9 %collective-permute-start.1 = (f32[2,128,512]{2,1,0:T(8,128)S(1)}, f32[2,128,512]{2,1,0:T(8,128)S(1)}, u32[]{:S(2)}, u32[]{:S(2)}) collective-permute-start(f32[2,128,512]{2,1,0:T(8,128)S(1)} %get-tuple-element.24), channel_id=1, source_target_pairs={{0,1},{1,0},{2,3},{3,2},{4,5},{5,4},{6,7},{7,6},{8,9},{9,8},{10,11... | collective-permute-start | bytes 1572872 | tf_op jit(solution)/shard_map/ppermute | solution.py:306
  1.5 15.7 %collective-permute-start.2 = (f32[2,128,512]{2,1,0:T(8,128)S(1)}, f32[2,128,512]{2,1,0:T(8,128)S(1)}, u32[]{:S(2)}, u32[]{:S(2)}) collective-permute-start(f32[2,128,512]{2,1,0:T(8,128)S(1)} %get-tuple-element.25), channel_id=1, source_target_pairs={{1,2},{2,1},{5,6},{6,5},{9,10},{10,9},{13,14},{14,13},{17,18},{18,... | collective-permute-start | bytes 1572872 | tf_op jit(solution)/shard_map/ppermute | solution.py:306
  6.9 24.4 %collective-permute-start.4 = (f32[2,512,128]{2,1,0:T(8,128)S(1)}, f32[2,512,128]{2,1,0:T(8,128)S(1)}, u32[]{:S(2)}, u32[]{:S(2)}) collective-permute-start(f32[2,512,128]{2,1,0:T(8,128)S(1)} %shard_map.77), channel_id=1, source_target_pairs={{0,4},{4,0},{8,12},{12,8},{16,20},{20,16},{24,28},{28,24},{1,5},{5... | collective-permute-start | bytes 1572872 | tf_op jit(solution)/shard_map/ppermute | solution.py:306
  17.2 14.1 %collective-permute-start.5 = (f32[2,2,128,128]{3,2,1,0:T(8,128)S(1)}, f32[2,2,128,128]{3,2,1,0:T(8,128)S(1)}, u32[]{:S(2)}, u32[]{:S(2)}) collective-permute-start(f32[2,2,128,128]{3,2,1,0:T(8,128)S(1)} %get-tuple-element.31), channel_id=1, source_target_pairs={{0,4},{4,0},{8,12},{12,8},{16,20},{20,16},{24,28},{28,24},{1,5},{5... | collective-permute-start | bytes 786440 | tf_op jit(solution)/shard_map/ppermute | solution.py:306
  19.9 19.2 %collective-permute-start = (f32[2,512,128]{2,1,0:T(8,128)S(1)}, f32[2,512,128]{2,1,0:T(8,128)S(1)}, u32[]{:S(2)}, u32[]{:S(2)}) collective-permute-start(f32[2,512,128]{2,1,0:T(8,128)S(1)} %shard_map.73), channel_id=1, source_target_pairs={{4,8},{12,16},{20,24},{8,4},{16,12},{24,20},{5,9},{13,17},{21,25},... | collective-permute-start | bytes 1572872 | tf_op jit(solution)/shard_map/ppermute | solution.py:306
  27.8 14.1 %collective-permute-start.3 = (f32[2,2,128,128]{3,2,1,0:T(8,128)S(1)}, f32[2,2,128,128]{3,2,1,0:T(8,128)S(1)}, u32[]{:S(2)}, u32[]{:S(2)}) collective-permute-start(f32[2,2,128,128]{3,2,1,0:T(8,128)S(1)} %get-tuple-element.26), channel_id=1, source_target_pairs={{4,8},{12,16},{20,24},{8,4},{16,12},{24,20},{5,9},{13,17},{21,25},... | collective-permute-start | bytes 786440 | tf_op jit(solution)/shard_map/ppermute | solution.py:306
  45.0 2.5 %collective-permute-start.7 = (f32[2,768,128]{2,1,0:T(8,128)S(1)}, f32[2,768,128]{2,1,0:T(8,128)S(1)}, u32[]{:S(2)}, u32[]{:S(2)}) collective-permute-start(f32[2,768,128]{2,1,0:T(8,128)S(1)} %get-tuple-element.38), channel_id=1, source_target_pairs={{0,4},{4,0},{8,12},{12,8},{16,20},{20,16},{24,28},{28,24},{1,5},{5... | collective-permute-start | bytes 2359304 | tf_op jit(solution)/shard_map/ppermute | solution.py:306
  47.6 13.2 %collective-permute-start.8 = (f32[2,4,128,128]{3,2,1,0:T(8,128)S(1)}, f32[2,4,128,128]{3,2,1,0:T(8,128)S(1)}, u32[]{:S(2)}, u32[]{:S(2)}) collective-permute-start(f32[2,4,128,128]{3,2,1,0:T(8,128)S(1)} %get-tuple-element.39), channel_id=1, source_target_pairs={{0,1},{1,0},{2,3},{3,2},{4,5},{5,4},{6,7},{7,6},{8,9},{9,8},{10,11... | collective-permute-start | bytes 1572872 | tf_op jit(solution)/shard_map/ppermute | solution.py:306
  47.7 15.0 %collective-permute-start.9 = (f32[2,4,128,128]{3,2,1,0:T(8,128)S(1)}, f32[2,4,128,128]{3,2,1,0:T(8,128)S(1)}, u32[]{:S(2)}, u32[]{:S(2)}) collective-permute-start(f32[2,4,128,128]{3,2,1,0:T(8,128)S(1)} %get-tuple-element.40), channel_id=1, source_target_pairs={{1,2},{2,1},{5,6},{6,5},{9,10},{10,9},{13,14},{14,13},{17,18},{18,... | collective-permute-start | bytes 1572872 | tf_op jit(solution)/shard_map/ppermute | solution.py:306
  49.6 22.1 %collective-permute-start.6 = (f32[2,512,128]{2,1,0:T(8,128)S(1)}, f32[2,512,128]{2,1,0:T(8,128)S(1)}, u32[]{:S(2)}, u32[]{:S(2)}) collective-permute-start(f32[2,512,128]{2,1,0:T(8,128)S(1)} %get-tuple-element.37), channel_id=1, source_target_pairs={{4,8},{12,16},{20,24},{8,4},{16,12},{24,20},{5,9},{13,17},{21,25},... | collective-permute-start | bytes 1572872 | tf_op jit(solution)/shard_map/ppermute | solution.py:306
  54.5 9.6 %collective-permute-start.10 = (f32[2,128,128]{2,1,0:T(8,128)S(1)}, f32[2,128,128]{2,1,0:T(8,128)S(1)}, u32[]{:S(2)}, u32[]{:S(2)}) collective-permute-start(f32[2,128,128]{2,1,0:T(8,128)S(1)} %get-tuple-element.41), channel_id=1, source_target_pairs={{4,9},{12,17},{20,25},{8,5},{16,13},{24,21},{5,8},{13,16},{21,24},... | collective-permute-start | bytes 393224 | tf_op jit(solution)/shard_map/ppermute | solution.py:306
  56.4 10.4 %collective-permute-start.11 = (f32[2,128,128]{2,1,0:T(8,128)S(1)}, f32[2,128,128]{2,1,0:T(8,128)S(1)}, u32[]{:S(2)}, u32[]{:S(2)}) collective-permute-start(f32[2,128,128]{2,1,0:T(8,128)S(1)} %get-tuple-element.42), channel_id=1, source_target_pairs={{5,10},{13,18},{21,26},{9,6},{17,14},{25,22},{6,9},{14,17},{22,25}... | collective-permute-start | bytes 393224 | tf_op jit(solution)/shard_map/ppermute | solution.py:306
